TPU v7x, 128 devices: a whole 4x4x4 slice. The times are simulated.
128 devices in a mesh: lat: 4 (over y_hi, core), lon: 32 (over x, z, y_lo).
Axes of the slice: x: 4, y: 4 (y_hi: 2, y_lo: 2; y = y_hi * 2 + y_lo), z: 4, core: 2. Of those that a mesh axis runs over, the one named last changes fastest.
Arguments:
- crm_state: bfloat16 [8, 1024, 58, 384], P('lat', 'lon'), may hold values from -4 to 4
- gcm_state: bfloat16 [8, 1024, 6, 72], P('lat', 'lon'), may hold values from -4 to 4
- micro_flags: int32 [8, 1024], P('lat', 'lon'), may hold values 0 or 1
- load_plan: int32 [8, 1024], P('lat', 'lon'), may hold values from 0 to 1023, as said below
- h_mix: bfloat16 [64, 64], replicated, may hold values from -0.75 to 0.75
- v_mix: bfloat16 [58, 58], replicated, may hold values from -0.75 to 0.75
- to_crm: float32 [58, 72], replicated, may hold values from -0.75 to 0.75
- to_gcm: float32 [72, 58], replicated, may hold values from -0.75 to 0.75
- polar_tracer: float32 [8, 72, 1024], P('lat', None, 'lon'), may hold values from -6 to 6
- courant_shift: int32 [8, 72], P('lat'), may hold values from 0 to 1023, as said below
- courant_frac: float32 [8, 72], P('lat'), may hold values from 0 to 1
Outputs:
- new_state: bfloat16 [8, 1024, 58, 384], P('lat', 'lon')
- tendency: float32 [8, 1024, 6, 72], P('lat', 'lon')
- polar_next: float32 [8, 72, 1024], P('lat', None, 'lon')
Inputs may be any that keep to these rules, and one draw needn't show every extreme that they name: Each row of load_plan is a permutation of the longitudes; of the 32 longitudes of one aligned block, exactly 1 map into each aligned block of 32 longitudes. `courant_shift`: displacements may be any number of whole cells around the loop; in every row at least one level is displaced by 512 to 543 cells.
All inputs are finite; a program needn't handle non-finite values. No bound on the sum of `micro_flags` on one device may be relied on, other than what follows from the above.
Results may differ from a plain program's by a relative error of at most 0.015.
Values may be sent and summed in bfloat16 or wider, within the bound.
A program may use at most 128 MiB of HBM per device.

v0:
```python
import jax
import jax.numpy as jnp
from jax import lax
from jax.sharding import PartitionSpec as P

NSUB = 18


def crm_advance(state_in, gcm_cols, flags, h_mix, v_mix, to_crm, to_gcm):
    count, levels, width = state_in.shape
    fields = gcm_cols.shape[1]
    columns = width // fields
    forcing = jnp.einsum(
        "lg,nfg->nlf", to_crm, gcm_cols.astype(jnp.float32), precision=lax.Precision.HIGHEST
    )
    start = state_in.astype(jnp.float32).reshape(count, levels, fields, columns)
    active = (flags == 1)[:, None, None]

    def substep(step, field_now):
        operand = field_now.astype(jnp.bfloat16)
        mixed = jnp.einsum(
            "nlfc,cd->nlfd", operand, h_mix, preferred_element_type=jnp.float32
        ).astype(jnp.bfloat16)
        lifted = jnp.einsum("ml,nlfd->nmfd", v_mix, mixed, preferred_element_type=jnp.float32)
        conversion = jnp.where(
            active,
            0.5 * jnp.tanh(field_now[:, :, 0] * field_now[:, :, 1]),
            -0.25 * field_now[:, :, 0],
        )
        adjust = jnp.concatenate(
            [
                conversion[:, :, None],
                -conversion[:, :, None],
                jnp.zeros((count, levels, fields - 2, columns), jnp.float32),
            ],
            axis=2,
        )
        return jnp.tanh(lifted) + 0.5 * forcing[..., None] + adjust

    final = lax.fori_loop(0, NSUB, substep, start)
    change = jnp.mean(final, axis=3) - jnp.mean(start, axis=3)
    tend = jnp.einsum("gl,nlf->nfg", to_gcm, change, precision=lax.Precision.HIGHEST)
    return (final.astype(jnp.bfloat16).reshape(count, levels, width), tend)


def pick_rows(values, picks):
    return jax.vmap(lambda row_vals, row_picks: row_vals[row_picks])(values, picks)


def per_device(
    crm_state,
    gcm_state,
    micro_flags,
    load_plan,
    h_mix,
    v_mix,
    to_crm,
    to_gcm,
    polar_tracer,
    courant_shift,
    courant_frac,
):
    rows_here, lon_cols, levels, width = crm_state.shape
    fields, glevels = (gcm_state.shape[2], gcm_state.shape[3])
    blocks = lax.axis_size("lon")
    per_pair = lon_cols // blocks
    my_index = lax.axis_index("lon")
    positions = jnp.arange(lon_cols, dtype=jnp.int32)
    dest_block = load_plan // lon_cols
    earlier = (dest_block[:, :, None] == dest_block[:, None, :]) & (
        positions[None, None, :] < positions[None, :, None]
    )
    send_slot = dest_block * per_pair + jnp.sum(earlier.astype(jnp.int32), axis=2)
    send_order = jnp.sum(
        positions[None, None, :]
        * (send_slot[:, None, :] == positions[None, :, None]).astype(jnp.int32),
        axis=2,
    )
    send_state = pick_rows(crm_state, send_order).reshape(
        rows_here, blocks, per_pair, levels, width
    )
    send_gcm = pick_rows(gcm_state, send_order).reshape(
        rows_here, blocks, per_pair, fields, glevels
    )
    send_flags = pick_rows(micro_flags, send_order).reshape(rows_here, blocks, per_pair)
    send_plan = pick_rows(load_plan, send_order).reshape(rows_here, blocks, per_pair)
    states = lax.all_to_all(send_state, "lon", split_axis=1, concat_axis=1, tiled=True)
    gcm_cols = lax.all_to_all(send_gcm, "lon", split_axis=1, concat_axis=1, tiled=True)
    flags = lax.all_to_all(send_flags, "lon", split_axis=1, concat_axis=1, tiled=True)
    plans = lax.all_to_all(send_plan, "lon", split_axis=1, concat_axis=1, tiled=True)
    items = states.shape[0]
    count = items * blocks * per_pair
    advanced, tend = crm_advance(
        states.reshape(count, levels, width),
        gcm_cols.reshape(count, fields, glevels),
        flags.reshape(count),
        h_mix,
        v_mix,
        to_crm,
        to_gcm,
    )
    advanced, tend_owner, plans_owner = (
        advanced.reshape(items, blocks, per_pair, levels, width),
        tend.reshape(items, blocks, per_pair, fields, glevels),
        plans,
    )
    owner_slot = plans_owner.reshape(rows_here, lon_cols) - my_index * lon_cols
    take_from = jnp.sum(
        positions[None, None, :]
        * (owner_slot[:, None, :] == positions[None, :, None]).astype(jnp.int32),
        axis=2,
    )
    new_state = pick_rows(advanced.reshape(rows_here, lon_cols, levels, width), take_from)
    returned = lax.all_to_all(tend_owner, "lon", split_axis=1, concat_axis=1, tiled=True).reshape(
        rows_here, lon_cols, fields, glevels
    )
    tendency = pick_rows(returned, send_slot)
    updated = polar_tracer + jnp.transpose(tendency[:, :, 0, :], (0, 2, 1))
    polar_cols = updated.shape[2]
    loop_cells = polar_cols * blocks
    weight = courant_frac[:, :, None]
    cells_here = jnp.arange(polar_cols, dtype=jnp.int32)
    whole = lax.all_gather(updated, "lon", axis=2, tiled=True)
    global_cells = my_index * polar_cols + cells_here
    first = (global_cells[None, None, :] - courant_shift[:, :, None]) % loop_cells
    second = (first - 1) % loop_cells
    upwind = jnp.take_along_axis(whole, first, axis=2)
    beyond = jnp.take_along_axis(whole, second, axis=2)
    polar_next = (1.0 - weight) * upwind + weight * beyond
    return (new_state, tendency, polar_next)


def solution(mesh):
    in_specs = (
        P("lat", "lon", None, None),
        P("lat", "lon", None, None),
        P("lat", "lon"),
        P("lat", "lon"),
        P(),
        P(),
        P(),
        P(),
        P("lat", None, "lon"),
        P("lat", None),
        P("lat", None),
    )
    out_specs = (P("lat", "lon", None, None), P("lat", "lon", None, None), P("lat", None, "lon"))
    return jax.shard_map(
        per_device, mesh=mesh, in_specs=in_specs, out_specs=out_specs, check_vma=False
    )
```

profile of v0, /device:TPU:16, one launch (start us, length us, event | category | flops | bytes accessed | tf_op | source)
XLA Modules:
  0.0 856.1 jit_solution(9885917399798235194)
XLA Ops:
  64.9 31.6 %all-to-all-done = bf16[2,32,1,58,384]{4,0,3,2,1:T(2,128)(2,1)} async-done(((bf16[2,32,1,58,384]{4,0,3,2,1:T(2,128)(2,1)}), bf16[2,32,1,58,384]{4,0,3,2,1:T(2,128)(2,1)}, u32[]{:S(2)}, u32[]{:S(2)}) %all-to-all-start) | async-done | bytes 2850848 | tf_op jit(solution)/shard_map/all_to_all | solution.py:87
  118.5 501.9 %while.10 = (s32[]{:T(128)}, f32[64,58,6,64]{1,3,2,0:T(8,128)}, bf16[64,64]{1,0:T(8,128)(2,1)S(1)}, bf16[58,58]{1,0:T(8,128)(2,1)S(1)}, f32[64,58,6]{1,2,0:T(8,1...) while((s32[]{:T(128)}, f32[64,58,6,64]{1,3,2,0:T(8,128)}, ...), condition=%wide.region_3.4_spmd, body=%wide.region_2.3_spmd.sunk | while | flops 357562112 | bytes 28790588 | solution.py:40
  134.5 11.9 %maximum_add_fusion.2 = f32[64,58,6,64]{1,3,2,0:T(8,128)} fusion(f32[64,58,1,64]{1,3,2,0:T(8,128)S(1)} %get-tuple-element.165, f32[64,58,1,64]{1,3,2,0:T(8,128)} %get-tuple-element.166, f32[6]{0:T(128)S(1)} %pad.2.clone.2, f32[64,58,6]{1,2,0:T(8,128)S(1)} %broadcast_multiply_fusion.2, f32[64,58,6,64]{1,3,2,0:T(8,128)} %copy.161, ...), kind=kOutput, calls=%fused_computation.8.clone.1 | convolution fusion | flops 356352000 | bytes 13407840 | tf_op jit(solution)/shard_map/while/body/eval_jaxpr/ml,nlfd->nmfd/dot_general | solution.py:24
  162.3 11.9 %maximum_add_fusion.2 = f32[64,58,6,64]{1,3,2,0:T(8,128)} fusion(f32[64,58,1,64]{1,3,2,0:T(8,128)S(1)} %get-tuple-element.165, f32[64,58,1,64]{1,3,2,0:T(8,128)} %get-tuple-element.166, f32[6]{0:T(128)S(1)} %pad.2.clone.2, f32[64,58,6]{1,2,0:T(8,128)S(1)} %broadcast_multiply_fusion.2, f32[64,58,6,64]{1,3,2,0:T(8,128)} %copy.161, ...), kind=kOutput, calls=%fused_computation.8.clone.1 | convolution fusion | flops 356352000 | bytes 13407840 | tf_op jit(solution)/shard_map/while/body/eval_jaxpr/ml,nlfd->nmfd/dot_general | solution.py:24
  190.2 11.9 %maximum_add_fusion.2 = f32[64,58,6,64]{1,3,2,0:T(8,128)} fusion(f32[64,58,1,64]{1,3,2,0:T(8,128)S(1)} %get-tuple-element.165, f32[64,58,1,64]{1,3,2,0:T(8,128)} %get-tuple-element.166, f32[6]{0:T(128)S(1)} %pad.2.clone.2, f32[64,58,6]{1,2,0:T(8,128)S(1)} %broadcast_multiply_fusion.2, f32[64,58,6,64]{1,3,2,0:T(8,128)} %copy.161, ...), kind=kOutput, calls=%fused_computation.8.clone.1 | convolution fusion | flops 356352000 | bytes 13407840 | tf_op jit(solution)/shard_map/while/body/eval_jaxpr/ml,nlfd->nmfd/dot_general | solution.py:24
  218.1 11.9 %maximum_add_fusion.2 = f32[64,58,6,64]{1,3,2,0:T(8,128)} fusion(f32[64,58,1,64]{1,3,2,0:T(8,128)S(1)} %get-tuple-element.165, f32[64,58,1,64]{1,3,2,0:T(8,128)} %get-tuple-element.166, f32[6]{0:T(128)S(1)} %pad.2.clone.2, f32[64,58,6]{1,2,0:T(8,128)S(1)} %broadcast_multiply_fusion.2, f32[64,58,6,64]{1,3,2,0:T(8,128)} %copy.161, ...), kind=kOutput, calls=%fused_computation.8.clone.1 | convolution fusion | flops 356352000 | bytes 13407840 | tf_op jit(solution)/shard_map/while/body/eval_jaxpr/ml,nlfd->nmfd/dot_general | solution.py:24
  246.0 11.9 %maximum_add_fusion.2 = f32[64,58,6,64]{1,3,2,0:T(8,128)} fusion(f32[64,58,1,64]{1,3,2,0:T(8,128)S(1)} %get-tuple-element.165, f32[64,58,1,64]{1,3,2,0:T(8,128)} %get-tuple-element.166, f32[6]{0:T(128)S(1)} %pad.2.clone.2, f32[64,58,6]{1,2,0:T(8,128)S(1)} %broadcast_multiply_fusion.2, f32[64,58,6,64]{1,3,2,0:T(8,128)} %copy.161, ...), kind=kOutput, calls=%fused_computation.8.clone.1 | convolution fusion | flops 356352000 | bytes 13407840 | tf_op jit(solution)/shard_map/while/body/eval_jaxpr/ml,nlfd->nmfd/dot_general | solution.py:24
  273.9 11.9 %maximum_add_fusion.2 = f32[64,58,6,64]{1,3,2,0:T(8,128)} fusion(f32[64,58,1,64]{1,3,2,0:T(8,128)S(1)} %get-tuple-element.165, f32[64,58,1,64]{1,3,2,0:T(8,128)} %get-tuple-element.166, f32[6]{0:T(128)S(1)} %pad.2.clone.2, f32[64,58,6]{1,2,0:T(8,128)S(1)} %broadcast_multiply_fusion.2, f32[64,58,6,64]{1,3,2,0:T(8,128)} %copy.161, ...), kind=kOutput, calls=%fused_computation.8.clone.1 | convolution fusion | flops 356352000 | bytes 13407840 | tf_op jit(solution)/shard_map/while/body/eval_jaxpr/ml,nlfd->nmfd/dot_general | solution.py:24
  301.8 11.9 %maximum_add_fusion.2 = f32[64,58,6,64]{1,3,2,0:T(8,128)} fusion(f32[64,58,1,64]{1,3,2,0:T(8,128)S(1)} %get-tuple-element.165, f32[64,58,1,64]{1,3,2,0:T(8,128)} %get-tuple-element.166, f32[6]{0:T(128)S(1)} %pad.2.clone.2, f32[64,58,6]{1,2,0:T(8,128)S(1)} %broadcast_multiply_fusion.2, f32[64,58,6,64]{1,3,2,0:T(8,128)} %copy.161, ...), kind=kOutput, calls=%fused_computation.8.clone.1 | convolution fusion | flops 356352000 | bytes 13407840 | tf_op jit(solution)/shard_map/while/body/eval_jaxpr/ml,nlfd->nmfd/dot_general | solution.py:24
  329.6 11.9 %maximum_add_fusion.2 = f32[64,58,6,64]{1,3,2,0:T(8,128)} fusion(f32[64,58,1,64]{1,3,2,0:T(8,128)S(1)} %get-tuple-element.165, f32[64,58,1,64]{1,3,2,0:T(8,128)} %get-tuple-element.166, f32[6]{0:T(128)S(1)} %pad.2.clone.2, f32[64,58,6]{1,2,0:T(8,128)S(1)} %broadcast_multiply_fusion.2, f32[64,58,6,64]{1,3,2,0:T(8,128)} %copy.161, ...), kind=kOutput, calls=%fused_computation.8.clone.1 | convolution fusion | flops 356352000 | bytes 13407840 | tf_op jit(solution)/shard_map/while/body/eval_jaxpr/ml,nlfd->nmfd/dot_general | solution.py:24
  357.5 11.9 %maximum_add_fusion.2 = f32[64,58,6,64]{1,3,2,0:T(8,128)} fusion(f32[64,58,1,64]{1,3,2,0:T(8,128)S(1)} %get-tuple-element.165, f32[64,58,1,64]{1,3,2,0:T(8,128)} %get-tuple-element.166, f32[6]{0:T(128)S(1)} %pad.2.clone.2, f32[64,58,6]{1,2,0:T(8,128)S(1)} %broadcast_multiply_fusion.2, f32[64,58,6,64]{1,3,2,0:T(8,128)} %copy.161, ...), kind=kOutput, calls=%fused_computation.8.clone.1 | convolution fusion | flops 356352000 | bytes 13407840 | tf_op jit(solution)/shard_map/while/body/eval_jaxpr/ml,nlfd->nmfd/dot_general | solution.py:24
  385.4 11.9 %maximum_add_fusion.2 = f32[64,58,6,64]{1,3,2,0:T(8,128)} fusion(f32[64,58,1,64]{1,3,2,0:T(8,128)S(1)} %get-tuple-element.165, f32[64,58,1,64]{1,3,2,0:T(8,128)} %get-tuple-element.166, f32[6]{0:T(128)S(1)} %pad.2.clone.2, f32[64,58,6]{1,2,0:T(8,128)S(1)} %broadcast_multiply_fusion.2, f32[64,58,6,64]{1,3,2,0:T(8,128)} %copy.161, ...), kind=kOutput, calls=%fused_computation.8.clone.1 | convolution fusion | flops 356352000 | bytes 13407840 | tf_op jit(solution)/shard_map/while/body/eval_jaxpr/ml,nlfd->nmfd/dot_general | solution.py:24
  413.3 11.9 %maximum_add_fusion.2 = f32[64,58,6,64]{1,3,2,0:T(8,128)} fusion(f32[64,58,1,64]{1,3,2,0:T(8,128)S(1)} %get-tuple-element.165, f32[64,58,1,64]{1,3,2,0:T(8,128)} %get-tuple-element.166, f32[6]{0:T(128)S(1)} %pad.2.clone.2, f32[64,58,6]{1,2,0:T(8,128)S(1)} %broadcast_multiply_fusion.2, f32[64,58,6,64]{1,3,2,0:T(8,128)} %copy.161, ...), kind=kOutput, calls=%fused_computation.8.clone.1 | convolution fusion | flops 356352000 | bytes 13407840 | tf_op jit(solution)/shard_map/while/body/eval_jaxpr/ml,nlfd->nmfd/dot_general | solution.py:24
  441.2 11.9 %maximum_add_fusion.2 = f32[64,58,6,64]{1,3,2,0:T(8,128)} fusion(f32[64,58,1,64]{1,3,2,0:T(8,128)S(1)} %get-tuple-element.165, f32[64,58,1,64]{1,3,2,0:T(8,128)} %get-tuple-element.166, f32[6]{0:T(128)S(1)} %pad.2.clone.2, f32[64,58,6]{1,2,0:T(8,128)S(1)} %broadcast_multiply_fusion.2, f32[64,58,6,64]{1,3,2,0:T(8,128)} %copy.161, ...), kind=kOutput, calls=%fused_computation.8.clone.1 | convolution fusion | flops 356352000 | bytes 13407840 | tf_op jit(solution)/shard_map/while/body/eval_jaxpr/ml,nlfd->nmfd/dot_general | solution.py:24
  469.1 11.9 %maximum_add_fusion.2 = f32[64,58,6,64]{1,3,2,0:T(8,128)} fusion(f32[64,58,1,64]{1,3,2,0:T(8,128)S(1)} %get-tuple-element.165, f32[64,58,1,64]{1,3,2,0:T(8,128)} %get-tuple-element.166, f32[6]{0:T(128)S(1)} %pad.2.clone.2, f32[64,58,6]{1,2,0:T(8,128)S(1)} %broadcast_multiply_fusion.2, f32[64,58,6,64]{1,3,2,0:T(8,128)} %copy.161, ...), kind=kOutput, calls=%fused_computation.8.clone.1 | convolution fusion | flops 356352000 | bytes 13407840 | tf_op jit(solution)/shard_map/while/body/eval_jaxpr/ml,nlfd->nmfd/dot_general | solution.py:24
  496.9 11.9 %maximum_add_fusion.2 = f32[64,58,6,64]{1,3,2,0:T(8,128)} fusion(f32[64,58,1,64]{1,3,2,0:T(8,128)S(1)} %get-tuple-element.165, f32[64,58,1,64]{1,3,2,0:T(8,128)} %get-tuple-element.166, f32[6]{0:T(128)S(1)} %pad.2.clone.2, f32[64,58,6]{1,2,0:T(8,128)S(1)} %broadcast_multiply_fusion.2, f32[64,58,6,64]{1,3,2,0:T(8,128)} %copy.161, ...), kind=kOutput, calls=%fused_computation.8.clone.1 | convolution fusion | flops 356352000 | bytes 13407840 | tf_op jit(solution)/shard_map/while/body/eval_jaxpr/ml,nlfd->nmfd/dot_general | solution.py:24
  524.8 11.9 %maximum_add_fusion.2 = f32[64,58,6,64]{1,3,2,0:T(8,128)} fusion(f32[64,58,1,64]{1,3,2,0:T(8,128)S(1)} %get-tuple-element.165, f32[64,58,1,64]{1,3,2,0:T(8,128)} %get-tuple-element.166, f32[6]{0:T(128)S(1)} %pad.2.clone.2, f32[64,58,6]{1,2,0:T(8,128)S(1)} %broadcast_multiply_fusion.2, f32[64,58,6,64]{1,3,2,0:T(8,128)} %copy.161, ...), kind=kOutput, calls=%fused_computation.8.clone.1 | convolution fusion | flops 356352000 | bytes 13407840 | tf_op jit(solution)/shard_map/while/body/eval_jaxpr/ml,nlfd->nmfd/dot_general | solution.py:24
  552.7 11.9 %maximum_add_fusion.2 = f32[64,58,6,64]{1,3,2,0:T(8,128)} fusion(f32[64,58,1,64]{1,3,2,0:T(8,128)S(1)} %get-tuple-element.165, f32[64,58,1,64]{1,3,2,0:T(8,128)} %get-tuple-element.166, f32[6]{0:T(128)S(1)} %pad.2.clone.2, f32[64,58,6]{1,2,0:T(8,128)S(1)} %broadcast_multiply_fusion.2, f32[64,58,6,64]{1,3,2,0:T(8,128)} %copy.161, ...), kind=kOutput, calls=%fused_computation.8.clone.1 | convolution fusion | flops 356352000 | bytes 13407840 | tf_op jit(solution)/shard_map/while/body/eval_jaxpr/ml,nlfd->nmfd/dot_general | solution.py:24
  580.6 11.9 %maximum_add_fusion.2 = f32[64,58,6,64]{1,3,2,0:T(8,128)} fusion(f32[64,58,1,64]{1,3,2,0:T(8,128)S(1)} %get-tuple-element.165, f32[64,58,1,64]{1,3,2,0:T(8,128)} %get-tuple-element.166, f32[6]{0:T(128)S(1)} %pad.2.clone.2, f32[64,58,6]{1,2,0:T(8,128)S(1)} %broadcast_multiply_fusion.2, f32[64,58,6,64]{1,3,2,0:T(8,128)} %copy.161, ...), kind=kOutput, calls=%fused_computation.8.clone.1 | convolution fusion | flops 356352000 | bytes 13407840 | tf_op jit(solution)/shard_map/while/body/eval_jaxpr/ml,nlfd->nmfd/dot_general | solution.py:24
  608.5 11.9 %maximum_add_fusion.2 = f32[64,58,6,64]{1,3,2,0:T(8,128)} fusion(f32[64,58,1,64]{1,3,2,0:T(8,128)S(1)} %get-tuple-element.165, f32[64,58,1,64]{1,3,2,0:T(8,128)} %get-tuple-element.166, f32[6]{0:T(128)S(1)} %pad.2.clone.2, f32[64,58,6]{1,2,0:T(8,128)S(1)} %broadcast_multiply_fusion.2, f32[64,58,6,64]{1,3,2,0:T(8,128)} %copy.161, ...), kind=kOutput, calls=%fused_computation.8.clone.1 | convolution fusion | flops 356352000 | bytes 13407840 | tf_op jit(solution)/shard_map/while/body/eval_jaxpr/ml,nlfd->nmfd/dot_general | solution.py:24
  620.4 14.6 %fusion.34 = (f32[64,58,6]{1,2,0:T(8,128)S(1)}, bf16[64,58,6,64]{1,3,2,0:T(8,128)(2,1)}) fusion(f32[64,58,6,64]{1,3,2,0:T(8,128)} %get-tuple-element.36), kind=kLoop, calls=%fused_computation.75 | loop fusion | flops 2828544 | bytes 8641536 | tf_op jit(solution)/shard_map/reduce_sum | solution.py:41
  661.1 87.6 %all_gather.3 = f32[2,72,1024]{1,2,0:T(8,128)S(1)} all-gather(f32[2,72,32]{1,2,0:T(8,128)S(1)} %fusion.20), channel_id=1, replica_groups=mesh['lat'=4,'lon'=32] {'lon'}, dimensions={2}, use_global_device_ids=true | all-gather | bytes 608256 | tf_op jit(solution)/shard_map/all_gather | solution.py:123
  749.7 35.5 %gather_fusion.7 = f32[4608]{0:T(1024)S(1)} fusion(f32[2,72,1024]{1,2,0:T(8,128)S(1)} %all_gather.3, s32[4608]{0:T(1024)S(1)} %reshape.196), kind=kCustom, calls=%fused_computation.1.clone | custom fusion | bytes 92160 | tf_op jit(solution)/shard_map/jit(take_along_axis)/gather | solution.py:128
  785.3 69.8 %gather_fusion.6 = f32[4608]{0:T(1024)S(1)} fusion(f32[2,72,1024]{1,2,0:T(8,128)} %copy-done.2, s32[4608]{0:T(1024)S(1)} %reshape.191), kind=kCustom, calls=%fused_computation.clone | custom fusion | bytes 92160 | tf_op jit(solution)/shard_map/jit(take_along_axis)/gather | solution.py:127
  (183 shorter events, 401.3 us)
Async XLA Ops:
  0.6 37.5 %copy-start = (bf16[2,32,58,384]{3,1,2,0:T(8,128)(2,1)S(1)}, bf16[2,32,58,384]{3,1,2,0:T(8,128)(2,1)}, u32[]{:S(2)}) copy-start(bf16[2,32,58,384]{3,1,2,0:T(8,128)(2,1)} %param.15) | copy-start | bytes 8552452
  0.6 25.2 %copy-start.3 = (bf16[2,32,6,72]{3,1,2,0:T(8,128)(2,1)S(1)}, bf16[2,32,6,72]{3,1,2,0:T(8,128)(2,1)}, u32[]{:S(2)}) copy-start(bf16[2,32,6,72]{3,1,2,0:T(8,128)(2,1)} %param.16) | copy-start | bytes 165892
  5.0 17.1 %all-to-all-start.2 = ((s32[2,32,1]{0,2,1:T(1,128)}), s32[2,32,1]{0,2,1:T(1,128)S(1)}, u32[]{:S(2)}, u32[]{:S(2)}) async-start(s32[2,32,1]{0,2,1:T(1,128)} %copy.119), calls=%async_computation.2 | async-start | bytes 32768 | tf_op jit(solution)/shard_map/all_to_all | solution.py:89
  22.0 12.0 %all-to-all-start.3 = ((s32[2,32,1]{0,2,1:T(1,128)}), s32[2,32,1]{0,2,1:T(1,128)S(1)}, u32[]{:S(2)}, u32[]{:S(2)}) async-start(s32[2,32,1]{0,2,1:T(1,128)} %copy.124), calls=%async_computation.3 | async-start | bytes 32768 | tf_op jit(solution)/shard_map/all_to_all | solution.py:90
  34.1 20.0 %all-to-all-start.1 = ((bf16[2,32,1,6,72]{4,0,3,2,1:T(2,128)(2,1)}), bf16[2,32,1,6,72]{4,0,3,2,1:T(2,128)(2,1)S(1)}, u32[]{:S(2)}, u32[]{:S(2)}) async-start(bf16[2,32,1,6,72]{4,0,3,2,1:T(2,128)(2,1)} %copy.117), calls=%async_computation.1 | async-start | bytes 196608 | tf_op jit(solution)/shard_map/all_to_all | solution.py:88
  54.1 8.7 %copy-start.9 = (s32[2,72]{1,0:T(2,128)S(1)}, s32[2,72]{1,0:T(2,128)}, u32[]{:S(2)}) copy-start(s32[2,72]{1,0:T(2,128)} %param.24) | copy-start | bytes 1732
  54.1 9.4 %copy-start.11 = (f32[2,72]{1,0:T(2,128)S(1)}, f32[2,72]{1,0:T(2,128)}, u32[]{:S(2)}) copy-start(f32[2,72]{1,0:T(2,128)} %param.25) | copy-start | bytes 1732
  54.1 10.4 %copy-start.6 = (f32[58,72]{1,0:T(8,128)S(1)}, f32[58,72]{1,0:T(8,128)}, u32[]{:S(2)}) copy-start(f32[58,72]{1,0:T(8,128)} %param.21) | copy-start | bytes 50116
  54.1 42.4 %all-to-all-start = ((bf16[2,32,1,58,384]{4,0,3,2,1:T(2,128)(2,1)}), bf16[2,32,1,58,384]{4,0,3,2,1:T(2,128)(2,1)}, u32[]{:S(2)}, u32[]{:S(2)}) async-start(bf16[2,32,1,58,384]{4,0,3,2,1:T(2,128)(2,1)} %copy.114), calls=%async_computation | async-start | bytes 5701632 | tf_op jit(solution)/shard_map/all_to_all | solution.py:87
  62.8 0.5 copy-start.14
  111.1 7.4 copy-start.4
  111.1 7.4 copy-start.5
  620.4 14.7 %copy-start.8 = (f32[72,58]{0,1:T(8,128)S(1)}, f32[72,58]{0,1:T(8,128)}, u32[]{:S(2)}) copy-start(f32[72,58]{0,1:T(8,128)} %param.22) | copy-start | bytes 50116
  636.2 23.3 %all-to-all-start.4 = ((f32[2,32,1,6,72]{4,0,3,2,1:T(2,128)}), f32[2,32,1,6,72]{4,0,3,2,1:T(2,128)S(1)}, u32[]{:S(2)}, u32[]{:S(2)}) async-start(f32[2,32,1,6,72]{4,0,3,2,1:T(2,128)} %copy.130), calls=%async_computation.4 | async-start | bytes 393216 | tf_op jit(solution)/shard_map/all_to_all | solution.py:114
  654.4 6.7 copy-start.7
  748.7 1.0 copy-start.2
  785.2 70.0 %copy-start.10 = (s32[2,72]{1,0:T(2,128)S(1)}, s32[2,72]{1,0:T(2,128)}, u32[]{:S(2)}) copy-start(s32[2,72]{1,0:T(2,128)} %param.24) | copy-start | bytes 1732
  785.2 70.0 %copy-start.12 = (f32[2,72]{1,0:T(2,128)S(1)}, f32[2,72]{1,0:T(2,128)}, u32[]{:S(2)}) copy-start(f32[2,72]{1,0:T(2,128)} %param.25) | copy-start | bytes 1732
  785.2 70.0 %copy-start.13 = (f32[2,72]{1,0:T(2,128)S(1)}, f32[2,72]{1,0:T(2,128)}, u32[]{:S(2)}) copy-start(f32[2,72]{1,0:T(2,128)} %broadcast_subtract_fusion) | copy-start | bytes 1732
  785.2 70.0 %copy-start.15 = (s32[32]{0:T(128)S(1)}, s32[32]{0:T(128)}, u32[]{:S(2)}) copy-start(s32[32]{0:T(128)} %copy-done.14) | copy-start | bytes 388
  785.2 70.9 %copy-start.1 = (bf16[2,32,58,384]{3,1,2,0:T(8,128)(2,1)S(1)}, bf16[2,32,58,384]{3,1,2,0:T(8,128)(2,1)}, u32[]{:S(2)}) copy-start(bf16[2,32,58,384]{3,1,2,0:T(8,128)(2,1)} %param.15) | copy-start | bytes 8552452
where the time goes:
time: 862 us; the launch traced here: 856 us
  local copies, waits for them, and re-layouts  374 us (43%)
  matrix products  215 us (25%)
  other arithmetic  103 us (12%)
  blocking collectives  87.6 us (10%)
  waiting for transfers between devices  43.9 us (5%)
  starting transfers between devices  31.8 us (4%)
    dot_general x18, matrix products, substep(): jnp.einsum('ml,nlfd->nmfd', v_mix, mixed, preferred_element_type=jnp.floa...  215 us
    while x18, local copies, waits for them, and re-layouts  213 us
    all_gather x1, blocking collectives, per_device(): whole = lax.all_gather(updated, 'lon', axis=2, tiled=True)  87.6 us
    neg x18, other arithmetic, substep(): -conversion[:, :, None]  72.2 us
    gather x3, local copies, waits for them, and re-layouts, per_device(): upwind = jnp.take_along_axis(whole, first, axis=2)  70 us
    gather x3, local copies, waits for them, and re-layouts, per_device(): beyond = jnp.take_along_axis(whole, second, axis=2)  35.7 us
    all_to_all x1, waiting for transfers between devices, per_device(): lax.all_to_all(send_state, 'lon', split_axis=1, concat_axis=1, tiled=True)  31.6 us
    reduce_sum x2, other arithmetic, crm_advance(): change = jnp.mean(final, axis=3) - jnp.mean(start, axis=3)  22 us
  transfers between devices with their start and end apart: 5, of which 3 were waited for; matrix products, arithmetic and copies ran while one was open for 5% of the time, Pallas kernels for 0%

commit v1 on v0

v1 whole, which is shorter than its diff:
```python
import functools

import jax
import jax.numpy as jnp
from jax import lax
from jax.experimental import pallas as pl
from jax.experimental.pallas import tpu as pltpu
from jax.sharding import PartitionSpec as P

NSUB = 18
MESH = pl.DeviceIdType.MESH
F32 = jnp.float32
BF16 = jnp.bfloat16
HIGHEST = lax.Precision.HIGHEST

SIZES = (4, 4, 2)


def _hops(off):
    return sum(min(d, n - d) for d, n in zip(off, SIZES))


OFFSETS = sorted(
    ((a, b, c) for a in range(4) for b in range(4) for c in range(2)),
    key=lambda off: (-_hops(off), off),
)
NBLK = len(OFFSETS)
CHUNKS = 4
PER = NBLK // CHUNKS
COLS = 2 * PER


def _shifted(me, off):
    x, z, y = me // 8, (me // 2) % 4, me % 2
    return ((x + off[0]) % 4) * 8 + ((z + off[1]) % 4) * 2 + (y + off[2]) % 2


def _pick(index, values):
    out = jnp.int32(values[0])
    for i, value in enumerate(values[1:], 1):
        out = jnp.where(index == i, jnp.int32(value), out)
    return out


def _iota(shape, axis):
    return lax.broadcasted_iota(jnp.int32, shape, axis)


def _dot(a, b, **kw):
    return jnp.dot(a, b, preferred_element_type=F32, **kw)


def _onehot(mask):
    return jnp.where(mask, jnp.float32(1), jnp.float32(0)).astype(BF16)


def advance(
    order,
    plan_s,
    flags,
    plan_v,
    crm,
    gcm,
    h_ref,
    v_ref,
    to_crm,
    to_gcm,
    tracer,
    recv,
    trec,
    prec,
    tbuf,
    crm_v,
    xa,
    xb,
    s0,
    fa,
    fb,
    gsc,
    hbd,
    vbd,
    ea,
    eb,
    ra,
    rb,
    tc,
    tg,
    sq,
    trt,
    updf,
    usend,
    snd,
    in_sem,
    self_sem,
    ssem,
    rsem,
    pssem,
    prsem,
    tssem,
    trsem,
):
    me = lax.axis_index("lon")
    load = pltpu.make_async_copy(crm, crm_v, in_sem)
    load.start()

    peers = [_shifted(me, off) for off in OFFSETS]
    barrier = pltpu.get_barrier_semaphore()
    for k in range(NBLK - 1):
        pl.semaphore_signal(barrier, inc=1, device_id={"lon": peers[k]}, device_id_type=MESH)

    tile_h = _onehot(_iota((64, 256), 1) % 64 == _iota((64, 256), 0))
    tile_ht = _onehot(_iota((256, 64), 0) % 64 == _iota((256, 64), 1))
    tile_v = _onehot(_iota((58, 256), 1) % 64 == _iota((58, 256), 0))
    tile_vt = _onehot(_iota((256, 58), 0) % 64 == _iota((256, 58), 1))
    diag = _iota((256, 256), 0) // 64 == _iota((256, 256), 1) // 64
    h_rep = _dot(_dot(tile_ht, h_ref[...]).astype(BF16), tile_h)
    v_rep = _dot(_dot(tile_vt, v_ref[...]).astype(BF16), tile_v)
    hbd[...] = jnp.where(diag, h_rep, 0.0).astype(BF16)
    vbd[...] = jnp.where(diag, v_rep, 0.0).astype(BF16)
    k_row, j_col = _iota((256, 256), 0) % 128, _iota((256, 256), 1)
    ea[...] = _onehot(k_row == j_col // 64)
    eb[...] = _onehot(k_row == jnp.where(j_col < 128, 4 + j_col // 64, 10 + j_col // 64))
    r_row, r_col = _iota((256, 128), 0), _iota((256, 128), 1)
    part = jnp.float32(1.0 / 64)
    ra[...] = jnp.where(r_col == r_row // 64, part, 0.0).astype(BF16)
    rb[...] = jnp.where(
        r_col == jnp.where(r_row < 128, 4 + r_row // 64, 10 + r_row // 64), part, 0.0
    ).astype(BF16)
    tc[...] = jnp.zeros_like(tc)
    tc[0:58, 0:72] = 0.5 * to_crm[...]
    tg[...] = jnp.zeros_like(tg)
    tg[0:72, 0:58] = to_gcm[...]
    gsc[...] = jnp.zeros_like(gsc)
    xa[...] = jnp.zeros_like(xa)
    xb[...] = jnp.zeros_like(xb)
    s0[...] = jnp.zeros_like(s0)
    for r in range(2):
        sq[...] = jnp.zeros_like(sq)
        sq[0:72, 0:32] = tracer[r]
        trt[r] = jnp.transpose(sq[...])[0:32, :]

    load.wait()
    pl.semaphore_wait(barrier, NBLK - 1)

    def plan_copy(k):
        return pltpu.make_async_remote_copy(
            src_ref=plan_v,
            dst_ref=prec.at[me],
            send_sem=pssem.at[k],
            recv_sem=prsem.at[k],
            device_id={"lon": peers[k]},
            device_id_type=MESH,
        )

    for k in range(NBLK - 1):
        plan_copy(k).start()
    own_plan = pltpu.make_async_copy(plan_v, prec.at[me], pssem.at[NBLK - 1])
    own_plan.start()

    low = _iota((64, 128), 1) < 64
    sgn = jnp.where(_iota((1, 128), 1) < 64, jnp.float32(1), jnp.float32(-1))

    def state_copy(k, dest):
        return pltpu.make_async_remote_copy(
            src_ref=snd.at[k],
            dst_ref=recv.at[me],
            send_sem=ssem.at[k],
            recv_sem=rsem.at[k],
            device_id={"lon": dest},
            device_id_type=MESH,
        )

    def chunk(ch, carry):
        dests = []
        for j in range(PER):
            offs = [OFFSETS[c * PER + j] for c in range(CHUNKS)]
            off = [_pick(ch, [o[i] for o in offs]) for i in range(3)]
            dests.append(_shifted(me, off))
        picks = [(r, order[r, dests[j]]) for j in range(PER) for r in range(2)]
        avs, bvs = [], []
        for c, (r, i) in enumerate(picks):
            half = pl.ds((c % 2) * 128, 128)
            column = crm_v[r, i]
            xa[c, 0:58, :] = column[:, 0:256]
            xb[c // 2, 0:58, half] = column[:, 256:384]
            s0[c, 0:58, :] = column[:, 0:128].astype(F32)
            gsc[c * 8 : c * 8 + 6, 0:72] = gcm[r, i].astype(F32)
            flag = flags[r, i]
            avs.append(sgn * jnp.where(flag == 1, jnp.float32(0.5), jnp.float32(0)))
            bvs.append(sgn * jnp.where(flag == 1, jnp.float32(0), jnp.float32(-0.25)))
        forcing = lax.dot_general(
            tc[...],
            gsc[...],
            (((1,), (1,)), ((), ())),
            precision=HIGHEST,
            preferred_element_type=F32,
        )
        for c in range(COLS):
            turned = forcing if c == 0 else pltpu.roll(forcing, 128 - 8 * c, 1)
            hi = turned.astype(BF16)
            lo = (turned - hi.astype(F32)).astype(BF16)
            both = jnp.concatenate([hi, lo], axis=1)
            fa[c] = _dot(both, ea[...])
            if c % 2 == 0:
                fb[c // 2] = _dot(both, eb[...])

        def substep(step, carry):
            h, v = hbd[...], vbd[...]
            for q in range(COLS // 4):
                x = xa[4 * q : 4 * q + 4].reshape(256, 256)
                mixed = _dot(x, h).astype(BF16)
                grown = jnp.tanh(_dot(v, mixed))
                for i in range(4):
                    c = 4 * q + i
                    new = grown[64 * i : 64 * i + 64] + fa[c]
                    old = s0[c]
                    turned = pltpu.roll(old, 64, 1)
                    adjust = (
                        jnp.tanh(old * turned) * avs[c] + jnp.where(low, old, turned) * bvs[c]
                    )
                    first = new[:, 0:128] + adjust
                    s0[c] = first
                    xa[c, :, 0:128] = first.astype(BF16)
                    xa[c, :, 128:256] = new[:, 128:256].astype(BF16)
            for q in range(COLS // 8):
                x = xb[4 * q : 4 * q + 4].reshape(256, 256)
                mixed = _dot(x, h).astype(BF16)
                grown = jnp.tanh(_dot(v, mixed))
                for i in range(4):
                    c = 4 * q + i
                    xb[c] = (grown[64 * i : 64 * i + 64] + fb[c]).astype(BF16)
            return carry

        lax.fori_loop(0, NSUB, substep, 0)

        total = jnp.zeros((64, 128), F32)
        for c, (r, i) in enumerate(picks):
            half = pl.ds((c % 2) * 128, 128)
            k = ch * PER + c // 2
            begun = crm_v[r, i]
            done_a, done_b = xa[c, 0:58, :], xb[c // 2, 0:58, half]
            snd[k, r, :, 0:256] = done_a
            snd[k, r, :, 256:384] = done_b
            xa[c, 0:58, :] = (done_a.astype(F32) - begun[:, 0:256].astype(F32)).astype(BF16)
            xb[c // 2, 0:58, half] = (done_b.astype(F32) - begun[:, 256:384].astype(F32)).astype(
                BF16
            )
            mean = _dot(xa[c], ra[...])
            total += mean if c == 0 else pltpu.roll(mean, 8 * c, 1)
            if c % 2 == 1:
                mean = _dot(xb[c // 2], rb[...])
                total += mean if c == 1 else pltpu.roll(mean, 8 * (c - 1), 1)
        tend = jnp.transpose(_dot(tg[...], total, precision=HIGHEST))
        for c in range(COLS):
            tbuf[dests[c // 2], c % 2] = tend[8 * c : 8 * c + 8]

        for j in range(PER - 1):
            state_copy(ch * PER + j, dests[j]).start()

        @pl.when(ch < CHUNKS - 1)
        def _():
            state_copy(ch * PER + PER - 1, dests[PER - 1]).start()

        return carry

    lax.fori_loop(0, CHUNKS, chunk, 0)

    own_state = pltpu.make_async_copy(snd.at[NBLK - 1], recv.at[me], self_sem)
    own_state.start()

    def row(i, carry):
        for r in range(2):
            updf[r, pl.ds(i, 1), :] = tbuf[plan_s[r, i] // 32, r, 0:1, :]
        return carry

    lax.fori_loop(0, 32, row, 0, unroll=8)
    usend[...] = (updf[...] + trt[...]).astype(BF16)

    def tracer_copy(k):
        return pltpu.make_async_remote_copy(
            src_ref=usend,
            dst_ref=trec.at[me],
            send_sem=tssem.at[k],
            recv_sem=trsem.at[k],
            device_id={"lon": peers[k]},
            device_id_type=MESH,
        )

    for k in range(NBLK - 1):
        tracer_copy(k).start()
    own_tracer = pltpu.make_async_copy(usend, trec.at[me], tssem.at[NBLK - 1])
    own_tracer.start()
    own_state.wait()
    own_plan.wait()
    own_tracer.wait()
    for k in range(NBLK - 1):
        plan_copy(k).wait()
        state_copy(k, peers[k]).wait()
        tracer_copy(k).wait()


def place(
    plan_s,
    recv,
    trec,
    prec,
    tbuf,
    shift,
    frac,
    state_out,
    tend_out,
    polar_out,
    rbuf,
    slots_v,
    slots_s,
    cs,
    cf,
    sq,
    in_sem,
    slot_sem,
    out_sem,
):
    me = lax.axis_index("lon")
    loads = [pltpu.make_async_copy(recv.at[pl.ds(8 * q, 8)], rbuf.at[pl.ds(8 * q, 8)], in_sem.at[q]) for q in range(4)]
    for load in loads:
        load.start()
    plans = prec[...]
    mine = jnp.where(plans // 32 == me, plans % 32, 0)
    slots_v[...] = jnp.broadcast_to(jnp.sum(mine, axis=2, keepdims=True), (32, 2, 128))
    to_smem = pltpu.make_async_copy(slots_v, slots_s, slot_sem)
    to_smem.start()
    to_smem.wait()
    for q in range(4):
        loads[q].wait()
        for s in range(8 * q, 8 * q + 8):
            for r in range(2):
                pltpu.make_async_copy(
                    rbuf.at[s, r], state_out.at[r, slots_s[s, r, 0]], out_sem.at[2 * s + r]
                ).start()

    for r in range(2):
        for i in range(32):
            tend_out[r, i] = tbuf[plan_s[r, i] // 32, r, 0:6, 0:72]

    cs[...] = jnp.zeros_like(cs)
    cf[...] = jnp.zeros_like(cf)
    cs[0:2, 0:72] = shift[...]
    cf[0:2, 0:72] = frac[...]
    for r in range(2):
        base = (me * 32 - 1 - cs[r : r + 1, :]) & 1023
        whole = trec[:, r].astype(F32).reshape(1024, 128)
        cut = jnp.concatenate([whole[512:1024], whole[0:32]], axis=0)
        now = jnp.where((base & 512) != 0, cut, whole[0:544])
        for size in (256, 128, 64, 32, 16, 8):
            rows = size + 32
            now = jnp.where((base & size) != 0, now[size : size + rows], now[0:rows])
        for size in (4, 2, 1):
            now = jnp.where((base & size) != 0, pltpu.roll(now, 40 - size, 0), now)
        weight = cf[r : r + 1, :]
        result = (1.0 - weight) * pltpu.roll(now, 39, 0) + weight * now
        sq[...] = jnp.zeros_like(sq)
        sq[0:32, :] = result[0:32]
        polar_out[r] = jnp.transpose(sq[...])[0:72, 0:32]

    for s in range(32):
        for r in range(2):
            pltpu.make_async_copy(
                rbuf.at[s, r], state_out.at[r, slots_s[s, r, 0]], out_sem.at[2 * s + r]
            ).wait()


def per_device(
    crm_state,
    gcm_state,
    micro_flags,
    load_plan,
    h_mix,
    v_mix,
    to_crm,
    to_gcm,
    polar_tracer,
    courant_shift,
    courant_frac,
):
    owners = load_plan // 32
    spots = jnp.arange(32, dtype=jnp.int32)
    order = jnp.sum(
        jnp.where(owners[:, None, :] == spots[None, :, None], spots[None, None, :], 0), axis=2
    )
    smem = pl.BlockSpec(memory_space=pltpu.SMEM)
    vmem = pl.BlockSpec(memory_space=pltpu.VMEM)
    hbm = pl.BlockSpec(memory_space=pl.ANY)
    recv, trec, prec, tbuf = pl.pallas_call(
        advance,
        out_shape=(
            jax.ShapeDtypeStruct((32, 2, 58, 384), BF16),
            jax.ShapeDtypeStruct((32, 2, 32, 128), BF16),
            jax.ShapeDtypeStruct((32, 2, 32), jnp.int32),
            jax.ShapeDtypeStruct((32, 2, 8, 128), F32),
        ),
        in_specs=[smem, smem, smem, vmem, hbm] + [vmem] * 6,
        out_specs=(hbm, hbm, hbm, vmem),
        scratch_shapes=[
            pltpu.VMEM((2, 32, 58, 384), BF16),
            pltpu.VMEM((COLS, 64, 256), BF16),
            pltpu.VMEM((COLS // 2, 64, 256), BF16),
            pltpu.VMEM((COLS, 64, 128), F32),
            pltpu.VMEM((COLS, 64, 256), F32),
            pltpu.VMEM((COLS // 2, 64, 256), F32),
            pltpu.VMEM((128, 128), F32),
            pltpu.VMEM((256, 256), BF16),
            pltpu.VMEM((256, 256), BF16),
            pltpu.VMEM((256, 256), BF16),
            pltpu.VMEM((256, 256), BF16),
            pltpu.VMEM((256, 128), BF16),
            pltpu.VMEM((256, 128), BF16),
            pltpu.VMEM((64, 128), F32),
            pltpu.VMEM((128, 64), F32),
            pltpu.VMEM((128, 128), F32),
            pltpu.VMEM((2, 32, 128), F32),
            pltpu.VMEM((2, 32, 128), F32),
            pltpu.VMEM((2, 32, 128), BF16),
            pltpu.VMEM((32, 2, 58, 384), BF16),
            pltpu.SemaphoreType.DMA,
            pltpu.SemaphoreType.DMA,
            pltpu.SemaphoreType.DMA((NBLK,)),
            pltpu.SemaphoreType.DMA((NBLK,)),
            pltpu.SemaphoreType.DMA((NBLK,)),
            pltpu.SemaphoreType.DMA((NBLK,)),
            pltpu.SemaphoreType.DMA((NBLK,)),
            pltpu.SemaphoreType.DMA((NBLK,)),
        ],
        compiler_params=pltpu.CompilerParams(collective_id=0, has_side_effects=True),
        name="advance",
    )(
        order,
        load_plan,
        micro_flags,
        load_plan,
        crm_state,
        gcm_state,
        h_mix,
        v_mix,
        to_crm,
        to_gcm,
        polar_tracer,
    )
    return pl.pallas_call(
        place,
        out_shape=(
            jax.ShapeDtypeStruct((2, 32, 58, 384), BF16),
            jax.ShapeDtypeStruct((2, 32, 6, 72), F32),
            jax.ShapeDtypeStruct((2, 72, 32), F32),
        ),
        in_specs=[smem, hbm] + [vmem] * 5,
        out_specs=(hbm, vmem, vmem),
        scratch_shapes=[
            pltpu.VMEM((32, 2, 58, 384), BF16),
            pltpu.VMEM((32, 2, 128), jnp.int32),
            pltpu.SMEM((32, 2, 128), jnp.int32),
            pltpu.VMEM((8, 128), jnp.int32),
            pltpu.VMEM((8, 128), F32),
            pltpu.VMEM((128, 128), F32),
            pltpu.SemaphoreType.DMA((4,)),
            pltpu.SemaphoreType.DMA,
            pltpu.SemaphoreType.DMA((64,)),
        ],
        name="place",
    )(load_plan, recv, trec, prec, tbuf, courant_shift, courant_frac)


def solution(mesh):
    in_specs = (
        P("lat", "lon", None, None),
        P("lat", "lon", None, None),
        P("lat", "lon"),
        P("lat", "lon"),
        P(),
        P(),
        P(),
        P(),
        P("lat", None, "lon"),
        P("lat", None),
        P("lat", None),
    )
    out_specs = (P("lat", "lon", None, None), P("lat", "lon", None, None), P("lat", None, "lon"))
    return jax.shard_map(
        per_device, mesh=mesh, in_specs=in_specs, out_specs=out_specs, check_vma=False
    )
```

time: 862 us -> 111 us (0.13)
  local copies, waits for them, and re-layouts: 374 us -> 15.7 us
  matrix products: 215 us -> 0 us
  other arithmetic: 103 us -> 1.37 us
  Pallas kernels: 0 us -> 92 us
  blocking collectives: 87.6 us -> 0 us
  waiting for transfers between devices: 43.9 us -> 0 us
  starting transfers between devices: 31.8 us -> 0 us
    while x20 -> x0, local copies, waits for them, and re-layouts: 223 us -> none
    dot_general x20 -> x0, matrix products: 215 us -> none  [the longest x18 215 us: substep(): jnp.einsum('ml,nlfd->nmfd', v_mix, mixed, preferred_element_type=jnp.floa...]
    gather x16 -> x0, local copies, waits for them, and re-layouts: 126 us -> none  [the longest x3 70 us: per_device(): upwind = jnp.take_along_axis(whole, first, axis=2)]
    pallas_call x0 -> x2, Pallas kernels: none -> 92 us  [the longest x1 86.4 us: per_device(): pl.pallas_call(advance, out_shape=(jax.ShapeDtypeStruct((32, 2, 58, 384),...]
    all_gather x1 -> x0, blocking collectives: 87.6 us -> none  [per_device(): whole = lax.all_gather(updated, 'lon', axis=2, tiled=True)]
    neg x18 -> x0, other arithmetic: 72.2 us -> none  [substep(): -conversion[:, :, None]]
    all_to_all x5 -> x0, waiting for transfers between devices: 43.9 us -> none  [the longest x1 31.6 us: per_device(): lax.all_to_all(send_state, 'lon', split_axis=1, concat_axis=1, tiled=True)]
    all_to_all x5 -> x0, starting transfers between devices: 31.8 us -> none  [the longest x1 8.88 us: per_device(): lax.all_to_all(send_flags, 'lon', split_axis=1, concat_axis=1, tiled=True)]
  transfers between devices with their start and end apart: 5 -> 0, of which waited for: 3 -> 0; matrix products, arithmetic and copies ran while one was open for 5% -> 0% of each run, Pallas kernels for 0% -> 0%
where the time goes in v1:
time: 111 us; the launch traced here: 110 us
  Pallas kernels  92 us (83%)
  local copies, waits for them, and re-layouts  15.7 us (14%)
  other arithmetic  1.37 us (1%)
    pallas_call x1, Pallas kernels, per_device(): pl.pallas_call(advance, out_shape=(jax.ShapeDtypeStruct((32, 2, 58, 384),...  86.4 us
    unnamed x8, local copies, waits for them, and re-layouts  9.11 us
    pallas_call x3, local copies, waits for them, and re-layouts, per_device(): pl.pallas_call(place, out_shape=(jax.ShapeDtypeStruct((2, 32, 58, 384), B...  6.58 us
    pallas_call x1, Pallas kernels, per_device(): pl.pallas_call(place, out_shape=(jax.ShapeDtypeStruct((2, 32, 58, 384), B...  5.53 us

profile of v1, /device:TPU:16, one launch (start us, length us, event | category | flops | bytes accessed | tf_op | source)
XLA Modules:
  0.0 109.7 jit_solution(15001534376066308168)
XLA Ops:
  0.6 0.7 and_select_fusion
  1.3 0.7 select_reduce_fusion.order
  2.0 1.5 %copy.23.to_gcm = f32[72,58]{1,0:T(8,128)} copy(f32[72,58]{0,1:T(8,128)} %param.18) | data formatting | bytes 33408 | tf_op args[7]
  3.5 1.5 %copy.24.tracer = f32[2,72,32]{2,1,0:T(8,128)} copy(f32[2,72,32]{1,2,0:T(8,128)} %param.19) | data formatting | bytes 36864 | tf_op args[8]
  4.9 1.6 %copy.22.gcm = bf16[2,32,6,72]{3,2,1,0:T(8,128)(2,1)} copy(bf16[2,32,6,72]{3,1,2,0:T(8,128)(2,1)} %param.12) | data formatting | bytes 110592 | tf_op args[1]
  6.5 4.6 %copy.21.crm = bf16[2,32,58,384]{3,2,1,0:T(8,128)(2,1)} copy(bf16[2,32,58,384]{3,1,2,0:T(8,128)(2,1)} %param.11) | data formatting | bytes 5701632 | tf_op args[0]
  11.1 86.4 %advance.1 = (bf16[32,2,58,384]{3,2,1,0:T(8,128)(2,1)}, bf16[32,2,32,128]{3,2,1,0:T(8,128)(2,1)}, s32[32,2,32]{2,1,0:T(2,128)}, f32[32,2,8,128]{3,2,1,0:T(8,128)}) custom-call(s32[2,32]{1,0:T(2,128)} %select_reduce_fusion.order, s32[2,32]{1,0:T(2,128)} %plan_s.3, s32[2,32]{1,0:T(2,128)} %flags.1, s32[2,32]{1,0:T(2,128)} %plan_s.3, ...), custom_call_target="tpu_custom_call" | custom-call | tf_op jit(solution)/shard_map/advance/pallas_call | solution.py:393
  97.6 5.5 %place.1 = (bf16[2,32,58,384]{3,2,1,0:T(8,128)(2,1)}, f32[2,32,6,72]{3,2,1,0:T(8,128)}, f32[2,72,32]{2,1,0:T(8,128)}) custom-call(s32[2,32]{1,0:T(2,128)} %plan_s.3, bf16[32,2,58,384]{3,2,1,0:T(8,128)(2,1)} %get-tuple-element.7.recv, bf16[32,2,32,128]{3,2,1,0:T(8,128)(2,1)} %get-tuple-element.8.trec, s32[32,2,32]{2,1,0:T(2,128)} %get-tuple-element.9.prec, ...), custom_call_target="tpu_custom_call" | custom-call | tf_op jit(solution)/shard_map/place/pallas_call | solution.py:448
  103.1 0.0 copy-start.1
  103.1 0.0 copy-start
  103.1 5.2 %copy.25 = bf16[2,32,58,384]{3,1,2,0:T(8,128)(2,1)} copy(bf16[2,32,58,384]{3,2,1,0:T(8,128)(2,1)} %get-tuple-element.14) | data formatting | bytes 5701632 | tf_op jit(solution)/shard_map/place/pallas_call | solution.py:448
  108.3 0.0 copy-done.1
  108.3 0.7 copy.27
  109.0 0.0 copy-done
  109.0 0.7 copy.26
Async XLA Ops:
  103.1 5.2 %copy-start.1 = (f32[2,72,32]{2,1,0:T(8,128)S(1)}, f32[2,72,32]{2,1,0:T(8,128)}, u32[]{:S(2)}) copy-start(f32[2,72,32]{2,1,0:T(8,128)} %get-tuple-element.16) | copy-start | bytes 55300
  103.1 5.9 %copy-start = (f32[2,32,6,72]{3,2,1,0:T(8,128)S(1)}, f32[2,32,6,72]{3,2,1,0:T(8,128)}, u32[]{:S(2)}) copy-start(f32[2,32,6,72]{3,2,1,0:T(8,128)} %get-tuple-element.15) | copy-start | bytes 331780

commit v2 on v1

v2 whole, which is shorter than its diff:
```python
import functools

import jax
import jax.numpy as jnp
from jax import lax
from jax.experimental import pallas as pl
from jax.experimental.pallas import tpu as pltpu
from jax.sharding import PartitionSpec as P

NSUB = 18
MESH = pl.DeviceIdType.MESH
F32 = jnp.float32
BF16 = jnp.bfloat16
HIGHEST = lax.Precision.HIGHEST

SIZES = (4, 4, 2)


def _hops(off):
    return sum(min(d, n - d) for d, n in zip(off, SIZES))


OFFSETS = sorted(
    ((a, b, c) for a in range(4) for b in range(4) for c in range(2)),
    key=lambda off: (-_hops(off), off),
)
NBLK = len(OFFSETS)
CHUNKS = 4
PER = NBLK // CHUNKS
GROUPS = ((0, 8, 1, 9), (2, 3, 10, 11), (4, 5, 12, 13))
UNROLL = 3
MERGE = 3
STEP = 33


def _shifted(me, off):
    x, z, y = me // 8, (me // 2) % 4, me % 2
    return ((x + off[0]) % 4) * 8 + ((z + off[1]) % 4) * 2 + (y + off[2]) % 2


def _pick(index, values):
    out = jnp.int32(values[0])
    for i, value in enumerate(values[1:], 1):
        out = jnp.where(index == i, jnp.int32(value), out)
    return out


def _iota(shape, axis):
    return lax.broadcasted_iota(jnp.int32, shape, axis)


def _dot(a, b, **kw):
    return jnp.dot(a, b, preferred_element_type=F32, **kw)


def _onehot(mask):
    return jnp.where(mask, jnp.float32(1), jnp.float32(0)).astype(BF16)


def _lane_map(quarter, lanes):
    out = jnp.full(quarter.shape, lanes[0], jnp.int32)
    for i, lane in enumerate(lanes[1:], 1):
        out = jnp.where(quarter == i, lane, out)
    return out


def advance(
    plan_s,
    flags,
    plan_v,
    crm,
    gcm,
    h_ref,
    v_ref,
    to_crm,
    to_gcm,
    tracer,
    recv,
    trec,
    prec,
    tbuf,
    crm_v,
    cn,
    xs,
    x0,
    s0,
    fs,
    lf,
    gn,
    gsc,
    hbd,
    vbd,
    spread,
    gather,
    tc,
    tg,
    trt,
    updf,
    usend,
    snd,
    order_v,
    order,
    in_sem,
    order_sem,
    self_sem,
    ssem,
    rsem,
    pssem,
    prsem,
    tssem,
    trsem,
):
    me = lax.axis_index("lon")
    loads = [pltpu.make_async_copy(crm.at[r], crm_v.at[r], in_sem.at[r]) for r in range(2)]
    for load in loads:
        load.start()

    peers = [_shifted(me, off) for off in OFFSETS]
    barrier = pltpu.get_barrier_semaphore()
    for k in range(NBLK - 1):
        pl.semaphore_signal(barrier, inc=1, device_id={"lon": peers[k]}, device_id_type=MESH)

    for r in range(2):
        owners = jnp.broadcast_to(plan_v[r : r + 1, :] // 32, (32, 32))
        at = jnp.where(owners == _iota((32, 32), 0), _iota((32, 32), 1), 0)
        order_v[r] = jnp.broadcast_to(jnp.max(at, axis=1, keepdims=True), (32, 128))
    to_smem = pltpu.make_async_copy(order_v, order, order_sem)
    to_smem.start()

    tile_h = _onehot(_iota((64, 256), 1) % 64 == _iota((64, 256), 0))
    tile_ht = _onehot(_iota((256, 64), 0) % 64 == _iota((256, 64), 1))
    tile_v = _onehot(_iota((58, 256), 1) % 64 == _iota((58, 256), 0))
    tile_vt = _onehot(_iota((256, 58), 0) % 64 == _iota((256, 58), 1))
    diag = _iota((256, 256), 0) // 64 == _iota((256, 256), 1) // 64
    h_rep = _dot(_dot(tile_ht, h_ref[...]).astype(BF16), tile_h)
    v_rep = _dot(_dot(tile_vt, v_ref[...]).astype(BF16), tile_v)
    hbd[...] = jnp.where(diag, h_rep, 0.0).astype(BF16)
    vbd[...] = jnp.where(diag, v_rep, 0.0).astype(BF16)
    for t, lanes in enumerate(GROUPS):
        spread[t] = _onehot(_iota((256, 256), 0) % 128 == _lane_map(_iota((256, 256), 1) // 64, lanes))
        hit = _iota((256, 128), 1) == _lane_map(_iota((256, 128), 0) // 64, lanes)
        gather[t * 256 : t * 256 + 256, :] = jnp.where(hit, jnp.float32(1.0 / 64), 0.0).astype(BF16)
    tc[...] = jnp.zeros_like(tc)
    tc[0:58, 0:72] = 0.5 * to_crm[...]
    tg[...] = jnp.zeros_like(tg)
    tg[0:58, 0:72] = to_gcm[...]
    gsc[...] = jnp.zeros_like(gsc)
    gn[...] = jnp.zeros_like(gn)
    xs[...] = jnp.zeros_like(xs)
    x0[...] = jnp.zeros_like(x0)
    s0[...] = jnp.zeros_like(s0)
    trt[...] = jnp.zeros_like(trt)
    for r in range(2):
        trt[r, :, 0:72] = tracer[r]
        for f in range(6):
            gn[(r * 6 + f) * STEP : (r * 6 + f) * STEP + 32, 0:72] = gcm[r, f].astype(F32)

    for r in range(2):
        loads[r].wait()

        def widen(level, carry):
            block = crm_v[r, level].astype(F32)
            for t in range(3):
                cn[t, pl.ds((r * 58 + level) * STEP, 32), :] = block[:, 128 * t : 128 * t + 128]
            return carry

        lax.fori_loop(0, 58, widen, 0, unroll=2)
    to_smem.wait()
    pl.semaphore_wait(barrier, NBLK - 1)

    def plan_copy(k):
        return pltpu.make_async_remote_copy(
            src_ref=plan_v,
            dst_ref=prec.at[me],
            send_sem=pssem.at[k],
            recv_sem=prsem.at[k],
            device_id={"lon": peers[k]},
            device_id_type=MESH,
        )

    for k in range(NBLK - 1):
        plan_copy(k).start()
    own_plan = pltpu.make_async_copy(plan_v, prec.at[me], pssem.at[NBLK - 1])
    own_plan.start()

    low58 = _iota((58, 128), 1) < 64
    low64 = _iota((64, 128), 1) < 64
    low1 = _iota((1, 128), 1) < 64

    def state_copy(k, dest):
        return pltpu.make_async_remote_copy(
            src_ref=snd.at[k],
            dst_ref=recv.at[me],
            send_sem=ssem.at[k],
            recv_sem=rsem.at[k],
            device_id={"lon": dest},
            device_id_type=MESH,
        )

    def chunk(ch, carry):
        dests = []
        for j in range(PER):
            offs = [OFFSETS[c * PER + j] for c in range(CHUNKS)]
            off = [_pick(ch, [o[i] for o in offs]) for i in range(3)]
            dests.append(_shifted(me, off))
        avs, bvs = [], []
        for p in range(PER):
            cols, a, b = [], [], []
            for r in range(2):
                i = order[r, dests[p], 0]
                cols.append([cn[t, pl.ds(r * 58 * STEP + i, 58, stride=STEP), :] for t in range(3)])
                row = 16 * p + 8 * r
                gsc[row : row + 6, :] = gn[pl.ds(r * 6 * STEP + i, 6, stride=STEP), :]
                flag = flags[r, i]
                a.append(jnp.where(flag == 1, jnp.float32(0.5), jnp.float32(0)))
                b.append(jnp.where(flag == 1, jnp.float32(0), jnp.float32(-0.25)))
            avs.append(jnp.where(low1, a[0], a[1]))
            bvs.append(jnp.where(low1, b[0], b[1]))
            one, two = cols[0][0], cols[1][0]
            first = jnp.where(low58, one, pltpu.roll(two, 64, 1))
            second = jnp.where(low58, pltpu.roll(one, 64, 1), two)
            s0[p, 0:58, 0:128] = first
            s0[p, 0:58, 128:256] = second
            blocks = ((first, second), (cols[0][1], cols[1][1]), (cols[0][2], cols[1][2]))
            for t in range(3):
                for half in range(2):
                    narrow = blocks[t][half].astype(BF16)
                    xs[t * PER + p, 0:58, 128 * half : 128 * half + 128] = narrow
                    x0[t * PER + p, 0:58, 128 * half : 128 * half + 128] = narrow
        forcing = lax.dot_general(
            tc[...],
            gsc[...],
            (((1,), (1,)), ((), ())),
            precision=HIGHEST,
            preferred_element_type=F32,
        )
        for p in range(PER):
            turned = forcing if p == 0 else pltpu.roll(forcing, 128 - 16 * p, 1)
            hi = turned.astype(BF16)
            lf[p, :, 0:128] = hi
            lf[p, :, 128:256] = (turned - hi.astype(F32)).astype(BF16)
        both = lf[...].reshape(PER * 64, 256)
        for t in range(3):
            fs[t * PER : t * PER + PER] = _dot(both, spread[t]).reshape(PER, 64, 256)

        def substep(step, carry):
            h, v = hbd[...], vbd[...]
            for m in range(0, 3 * PER // 4, MERGE):
                x = xs[4 * m : 4 * (m + MERGE)].reshape(MERGE * 256, 256)
                all_mixed = _dot(x, h).astype(BF16)
                for q in range(m, m + MERGE):
                    mixed = all_mixed[256 * (q - m) : 256 * (q - m) + 256]
                    grown = jnp.tanh(_dot(v, mixed))
                    for i in range(4):
                        c = 4 * q + i
                        new = grown[64 * i : 64 * i + 64] + fs[c]
                        if c < PER:
                            one, two = s0[c, :, 0:128], s0[c, :, 128:256]
                            adjust = jnp.tanh(one * two) * avs[c] + one * bvs[c]
                            first, second = new[:, 0:128] + adjust, new[:, 128:256] - adjust
                            s0[c, :, 0:128] = first
                            s0[c, :, 128:256] = second
                            xs[c, :, 0:128] = first.astype(BF16)
                            xs[c, :, 128:256] = second.astype(BF16)
                        else:
                            xs[c] = new.astype(BF16)
            return carry

        lax.fori_loop(0, NSUB, substep, 0, unroll=UNROLL)

        for p in range(PER):
            k = ch * PER + p
            one, two = s0[p, :, 0:128], s0[p, :, 128:256]
            left = jnp.where(low64, one, pltpu.roll(two, 64, 1)).astype(BF16)
            right = jnp.where(low64, pltpu.roll(one, 64, 1), two).astype(BF16)
            snd[k, 0, :, 0:128] = left[0:58]
            snd[k, 1, :, 0:128] = right[0:58]
            for t in (1, 2):
                for r in range(2):
                    snd[k, r, :, 128 * t : 128 * t + 128] = xs[
                        t * PER + p, 0:58, 128 * r : 128 * r + 128
                    ]
        mean = jnp.zeros((PER * 64, 128), F32)
        for t in range(3):
            diff = (xs[t * PER : t * PER + PER] - x0[t * PER : t * PER + PER]).reshape(PER * 64, 256)
            mean += _dot(diff, gather[t * 256 : t * 256 + 256, :])
        total = mean[0:64]
        for p in range(1, PER):
            total += pltpu.roll(mean[64 * p : 64 * p + 64], 16 * p, 1)
        tend = _dot(jnp.transpose(total), tg[...], precision=HIGHEST)
        for p in range(PER):
            for r in range(2):
                row = 16 * p + 8 * r
                tbuf[dests[p], r] = tend[row : row + 8]

        for j in range(PER - 1):
            state_copy(ch * PER + j, dests[j]).start()

        @pl.when(ch < CHUNKS - 1)
        def _():
            state_copy(ch * PER + PER - 1, dests[PER - 1]).start()

        return carry

    lax.fori_loop(0, CHUNKS, chunk, 0)

    own_state = pltpu.make_async_copy(snd.at[NBLK - 1], recv.at[me], self_sem)
    own_state.start()

    def row(i, carry):
        for r in range(2):
            updf[r, pl.ds(i, 1), :] = tbuf[plan_s[r, i] // 32, r, 0:1, :]
        return carry

    lax.fori_loop(0, 32, row, 0, unroll=8)
    usend[...] = (updf[...] + trt[...]).astype(BF16)

    def tracer_copy(k):
        return pltpu.make_async_remote_copy(
            src_ref=usend,
            dst_ref=trec.at[me],
            send_sem=tssem.at[k],
            recv_sem=trsem.at[k],
            device_id={"lon": peers[k]},
            device_id_type=MESH,
        )

    for k in range(NBLK - 1):
        tracer_copy(k).start()
    own_tracer = pltpu.make_async_copy(usend, trec.at[me], tssem.at[NBLK - 1])
    own_tracer.start()
    own_state.wait()
    own_plan.wait()
    own_tracer.wait()
    for k in range(NBLK - 1):
        plan_copy(k).wait()
        state_copy(k, peers[k]).wait()
        tracer_copy(k).wait()


def place(
    plan_s,
    recv,
    trec,
    prec,
    tbuf,
    shift,
    frac,
    state_out,
    tend_out,
    polar_out,
    rbuf,
    wide,
    obuf,
    tn,
    slots_v,
    slots_s,
    cs,
    cf,
    in_sem,
    slot_sem,
    out_sem,
):
    me = lax.axis_index("lon")
    loads = [
        pltpu.make_async_copy(recv.at[pl.ds(8 * q, 8)], rbuf.at[pl.ds(8 * q, 8)], in_sem.at[q])
        for q in range(4)
    ]
    for load in loads:
        load.start()
    plans = prec[...]
    mine = jnp.where(plans // 32 == me, plans % 32, 0)
    slots_v[...] = jnp.broadcast_to(jnp.max(mine, axis=2, keepdims=True), (32, 2, 128))
    to_smem = pltpu.make_async_copy(slots_v, slots_s, slot_sem)
    to_smem.start()

    for r in range(2):
        for i in range(32):
            tn[pl.ds(r * 6 * STEP + i, 6, stride=STEP), :] = tbuf[plan_s[r, i] // 32, r, 0:6, :]
        for f in range(6):
            at = (r * 6 + f) * STEP
            tend_out[r, f] = tn[at : at + 32, 0:72]

    cs[...] = jnp.zeros_like(cs)
    cf[...] = jnp.zeros_like(cf)
    cs[0:2, 0:72] = shift[...]
    cf[0:2, 0:72] = frac[...]
    for r in range(2):
        base = (me * 32 - 1 - cs[r : r + 1, :]) & 1023
        whole = trec[:, r].astype(F32).reshape(1024, 128)
        cut = jnp.concatenate([whole[512:1024], whole[0:32]], axis=0)
        now = jnp.where((base & 512) != 0, cut, whole[0:544])
        for size in (256, 128, 64, 32, 16, 8):
            rows = size + 32
            now = jnp.where((base & size) != 0, now[size : size + rows], now[0:rows])
        for size in (4, 2, 1):
            now = jnp.where((base & size) != 0, pltpu.roll(now, 40 - size, 0), now)
        weight = cf[r : r + 1, :]
        result = (1.0 - weight) * pltpu.roll(now, 39, 0) + weight * now
        polar_out[r] = result[0:32, 0:72]

    to_smem.wait()
    for q in range(4):
        loads[q].wait()

        def spot(s, carry):
            for r in range(2):
                column = rbuf[s, r].astype(F32)
                at = pl.ds(r * 58 * STEP + slots_s[s, r, 0], 58, stride=STEP)
                for t in range(3):
                    wide[t, at, :] = column[:, 128 * t : 128 * t + 128]
            return carry

        lax.fori_loop(8 * q, 8 * q + 8, spot, 0, unroll=2)

    outs = []
    for r in range(2):
        for part in range(2):

            def narrow(level, carry):
                for t in range(3):
                    obuf[r, level, :, 128 * t : 128 * t + 128] = wide[
                        t, pl.ds((r * 58 + level) * STEP, 32), :
                    ].astype(BF16)
                return carry

            lax.fori_loop(29 * part, 29 * part + 29, narrow, 0, unroll=True)
            piece = pl.ds(29 * part, 29)
            outs.append(
                pltpu.make_async_copy(
                    obuf.at[r, piece], state_out.at[r, piece], out_sem.at[2 * r + part]
                )
            )
            outs[-1].start()
    for out in outs:
        out.wait()


def per_device(
    crm_state,
    gcm_state,
    micro_flags,
    load_plan,
    h_mix,
    v_mix,
    to_crm,
    to_gcm,
    polar_tracer,
    courant_shift,
    courant_frac,
):
    smem = pl.BlockSpec(memory_space=pltpu.SMEM)
    vmem = pl.BlockSpec(memory_space=pltpu.VMEM)
    hbm = pl.BlockSpec(memory_space=pl.ANY)
    dma = pltpu.SemaphoreType.DMA
    recv, trec, prec, tbuf = pl.pallas_call(
        advance,
        out_shape=(
            jax.ShapeDtypeStruct((32, 2, 58, 384), BF16),
            jax.ShapeDtypeStruct((32, 2, 32, 128), BF16),
            jax.ShapeDtypeStruct((32, 2, 32), jnp.int32),
            jax.ShapeDtypeStruct((32, 2, 8, 128), F32),
        ),
        in_specs=[smem, smem, vmem, hbm] + [vmem] * 6,
        out_specs=(hbm, hbm, hbm, vmem),
        scratch_shapes=[
            pltpu.VMEM((2, 58, 32, 384), BF16),
            pltpu.VMEM((3, 2 * 58 * STEP, 128), F32),
            pltpu.VMEM((3 * PER, 64, 256), BF16),
            pltpu.VMEM((3 * PER, 64, 256), BF16),
            pltpu.VMEM((PER, 64, 256), F32),
            pltpu.VMEM((3 * PER, 64, 256), F32),
            pltpu.VMEM((PER, 64, 256), BF16),
            pltpu.VMEM((2 * 6 * STEP, 128), F32),
            pltpu.VMEM((128, 128), F32),
            pltpu.VMEM((256, 256), BF16),
            pltpu.VMEM((256, 256), BF16),
            pltpu.VMEM((3, 256, 256), BF16),
            pltpu.VMEM((768, 128), BF16),
            pltpu.VMEM((64, 128), F32),
            pltpu.VMEM((64, 128), F32),
            pltpu.VMEM((2, 32, 128), F32),
            pltpu.VMEM((2, 32, 128), F32),
            pltpu.VMEM((2, 32, 128), BF16),
            pltpu.VMEM((32, 2, 58, 384), BF16),
            pltpu.VMEM((2, 32, 128), jnp.int32),
            pltpu.SMEM((2, 32, 128), jnp.int32),
            dma((2,)),
            dma,
            dma,
            dma((NBLK,)),
            dma((NBLK,)),
            dma((NBLK,)),
            dma((NBLK,)),
            dma((NBLK,)),
            dma((NBLK,)),
        ],
        compiler_params=pltpu.CompilerParams(collective_id=0, has_side_effects=True),
        name="advance",
    )(
        load_plan,
        micro_flags,
        load_plan,
        jnp.transpose(crm_state, (0, 2, 1, 3)),
        jnp.transpose(gcm_state, (0, 2, 1, 3)),
        h_mix,
        v_mix,
        to_crm,
        to_gcm.T,
        jnp.transpose(polar_tracer, (0, 2, 1)),
    )
    new_state, tendency, polar_next = pl.pallas_call(
        place,
        out_shape=(
            jax.ShapeDtypeStruct((2, 58, 32, 384), BF16),
            jax.ShapeDtypeStruct((2, 6, 32, 72), F32),
            jax.ShapeDtypeStruct((2, 32, 72), F32),
        ),
        in_specs=[smem, hbm] + [vmem] * 5,
        out_specs=(hbm, vmem, vmem),
        scratch_shapes=[
            pltpu.VMEM((32, 2, 58, 384), BF16),
            pltpu.VMEM((3, 2 * 58 * STEP, 128), F32),
            pltpu.VMEM((2, 58, 32, 384), BF16),
            pltpu.VMEM((2 * 6 * STEP, 128), F32),
            pltpu.VMEM((32, 2, 128), jnp.int32),
            pltpu.SMEM((32, 2, 128), jnp.int32),
            pltpu.VMEM((8, 128), jnp.int32),
            pltpu.VMEM((8, 128), F32),
            dma((4,)),
            dma,
            dma((4,)),
        ],
        name="place",
    )(load_plan, recv, trec, prec, tbuf, courant_shift, courant_frac)
    return (
        jnp.transpose(new_state, (0, 2, 1, 3)),
        jnp.transpose(tendency, (0, 2, 1, 3)),
        jnp.transpose(polar_next, (0, 2, 1)),
    )


def solution(mesh):
    in_specs = (
        P("lat", "lon", None, None),
        P("lat", "lon", None, None),
        P("lat", "lon"),
        P("lat", "lon"),
        P(),
        P(),
        P(),
        P(),
        P("lat", None, "lon"),
        P("lat", None),
        P("lat", None),
    )
    out_specs = (P("lat", "lon", None, None), P("lat", "lon", None, None), P("lat", None, "lon"))
    return jax.shard_map(
        per_device, mesh=mesh, in_specs=in_specs, out_specs=out_specs, check_vma=False
    )
```

time: 111 us -> 76.2 us (0.69)
  Pallas kernels: 92 us -> 75 us
  local copies, waits for them, and re-layouts: 15.7 us -> 0 us
  other arithmetic: 1.37 us -> 0 us
    pallas_call x1, Pallas kernels: 86.4 us -> 69.1 us  [per_device(): pl.pallas_call(advance, out_shape=(jax.ShapeDtypeStruct((32, 2, 58, 384),...]
    unnamed x8 -> x0, local copies, waits for them, and re-layouts: 9.11 us -> none
    pallas_call x3 -> x0, local copies, waits for them, and re-layouts: 6.58 us -> none  [per_device(): pl.pallas_call(place, out_shape=(jax.ShapeDtypeStruct((2, 32, 58, 384), B...]
where the time goes in v2:
time: 76.2 us; the launch traced here: 75.6 us
  Pallas kernels  75 us (98%)
    pallas_call x1, Pallas kernels, per_device(): pl.pallas_call(advance, out_shape=(jax.ShapeDtypeStruct((32, 2, 58, 384),...  69.1 us
    pallas_call x1, Pallas kernels, per_device(): pl.pallas_call(place, out_shape=(jax.ShapeDtypeStruct((2, 58, 32, 384), B...  5.86 us

profile of v2, /device:TPU:16, one launch (start us, length us, event | category | flops | bytes accessed | tf_op | source)
XLA Modules:
  0.0 75.6 jit_solution(17835987533476277554)
XLA Ops:
  0.6 69.1 %advance.1 = (bf16[32,2,58,384]{3,2,1,0:T(8,128)(2,1)}, bf16[32,2,32,128]{3,2,1,0:T(8,128)(2,1)}, s32[32,2,32]{2,1,0:T(2,128)}, f32[32,2,8,128]{3,2,1,0:T(8,128)}) custom-call(s32[2,32]{1,0:T(2,128)} %plan_s.3, s32[2,32]{1,0:T(2,128)} %flags.1, s32[2,32]{1,0:T(2,128)} %plan_s.3, bf16[2,58,32,384]{3,2,1,0:T(8,128)(2,1)} %bitcast.7, ...), custom_call_target="tpu_custom_call" | custom-call | tf_op jit(solution)/shard_map/advance/pallas_call | solution.py:456
  69.8 5.9 %place.1 = (bf16[2,58,32,384]{3,2,1,0:T(8,128)(2,1)}, f32[2,6,32,72]{3,2,1,0:T(8,128)}, f32[2,32,72]{2,1,0:T(8,128)}) custom-call(s32[2,32]{1,0:T(2,128)} %plan_s.3, bf16[32,2,58,384]{3,2,1,0:T(8,128)(2,1)} %get-tuple-element.10.recv, bf16[32,2,32,128]{3,2,1,0:T(8,128)(2,1)} %get-tuple-element.11.trec, s32[32,2,32]{2,1,0:T(2,128)} %get-tuple-element.12.prec, ...), custom_call_target="tpu_custom_call" | custom-call | tf_op jit(solution)/shard_map/place/pallas_call | solution.py:512

commit v3 on v2

--- a/solution.py
+++ b/solution.py
@@ -28,7 +28,7 @@
 CHUNKS = 4
 PER = NBLK // CHUNKS
 GROUPS = ((0, 8, 1, 9), (2, 3, 10, 11), (4, 5, 12, 13))
-UNROLL = 3
+UNROLL = 18
 MERGE = 3
 STEP = 33
 
@@ -65,7 +65,6 @@
 
 
 def advance(
-    plan_s,
     flags,
     plan_v,
     crm,
@@ -98,6 +97,7 @@
     updf,
     usend,
     snd,
+    pack,
     order_v,
     order,
     in_sem,
@@ -124,6 +124,15 @@
         owners = jnp.broadcast_to(plan_v[r : r + 1, :] // 32, (32, 32))
         at = jnp.where(owners == _iota((32, 32), 0), _iota((32, 32), 1), 0)
         order_v[r] = jnp.broadcast_to(jnp.max(at, axis=1, keepdims=True), (32, 128))
+    lane = _iota((1, 128), 1)
+    bound = jnp.full((1, 128), 64, jnp.int32)
+    for k in range(NBLK):
+        bound = jnp.where(lane // 2 == k, peers[k], bound)
+    value = jnp.where(_iota((32, 128), 1) % 2 == 0, order_v[0], order_v[1] + 32)
+    spot = jnp.where(bound == _iota((32, 128), 0), value, 0)
+    pack[...] = jnp.zeros_like(pack)
+    pack[0:2, 0:32] = plan_v[...]
+    pack[2:3, :] = jnp.max(spot, axis=0, keepdims=True)
     to_smem = pltpu.make_async_copy(order_v, order, order_sem)
     to_smem.start()
 
@@ -166,11 +175,10 @@
 
         lax.fori_loop(0, 58, widen, 0, unroll=2)
     to_smem.wait()
-    pl.semaphore_wait(barrier, NBLK - 1)
-
-    def plan_copy(k):
+
+    def pack_copy(k):
         return pltpu.make_async_remote_copy(
-            src_ref=plan_v,
+            src_ref=pack,
             dst_ref=prec.at[me],
             send_sem=pssem.at[k],
             recv_sem=prsem.at[k],
@@ -178,10 +186,21 @@
             device_id_type=MESH,
         )
 
-    for k in range(NBLK - 1):
-        plan_copy(k).start()
-    own_plan = pltpu.make_async_copy(plan_v, prec.at[me], pssem.at[NBLK - 1])
-    own_plan.start()
+    own_pack = pltpu.make_async_copy(pack, prec.at[me], pssem.at[NBLK - 1])
+    own_pack.start()
+
+    def tracer_copy(ch, k):
+        return pltpu.make_async_remote_copy(
+            src_ref=usend.at[ch],
+            dst_ref=trec.at[me, ch],
+            send_sem=tssem.at[ch, k],
+            recv_sem=trsem.at[ch, k],
+            device_id={"lon": peers[k]},
+            device_id_type=MESH,
+        )
+
+    def own_tracer(ch):
+        return pltpu.make_async_copy(usend.at[ch], trec.at[me, ch], tssem.at[ch, NBLK - 1])
 
     low58 = _iota((58, 128), 1) < 64
     low64 = _iota((64, 128), 1) < 64
@@ -268,6 +287,22 @@
 
         lax.fori_loop(0, NSUB, substep, 0, unroll=UNROLL)
 
+        mean = jnp.zeros((PER * 64, 128), F32)
+        for t in range(3):
+            diff = (xs[t * PER : t * PER + PER] - x0[t * PER : t * PER + PER]).reshape(PER * 64, 256)
+            mean += _dot(diff, gather[t * 256 : t * 256 + 256, :])
+        total = mean[0:64]
+        for p in range(1, PER):
+            total += pltpu.roll(mean[64 * p : 64 * p + 64], 16 * p, 1)
+        tend = _dot(jnp.transpose(total), tg[...], precision=HIGHEST)
+        for p in range(PER):
+            for r in range(2):
+                row = 16 * p + 8 * r
+                tbuf[dests[p], r] = tend[row : row + 8]
+                home = pl.ds(order[r, dests[p], 0], 1)
+                updf[2 * p + r : 2 * p + r + 1, :] = tend[row : row + 1] + trt[r, home, :]
+        usend[ch] = updf[...].astype(BF16)
+
         for p in range(PER):
             k = ch * PER + p
             one, two = s0[p, :, 0:128], s0[p, :, 128:256]
@@ -280,19 +315,16 @@
                     snd[k, r, :, 128 * t : 128 * t + 128] = xs[
                         t * PER + p, 0:58, 128 * r : 128 * r + 128
                     ]
-        mean = jnp.zeros((PER * 64, 128), F32)
-        for t in range(3):
-            diff = (xs[t * PER : t * PER + PER] - x0[t * PER : t * PER + PER]).reshape(PER * 64, 256)
-            mean += _dot(diff, gather[t * 256 : t * 256 + 256, :])
-        total = mean[0:64]
-        for p in range(1, PER):
-            total += pltpu.roll(mean[64 * p : 64 * p + 64], 16 * p, 1)
-        tend = _dot(jnp.transpose(total), tg[...], precision=HIGHEST)
-        for p in range(PER):
-            for r in range(2):
-                row = 16 * p + 8 * r
-                tbuf[dests[p], r] = tend[row : row + 8]
-
+
+        @pl.when(ch == 0)
+        def _():
+            pl.semaphore_wait(barrier, NBLK - 1)
+            for k in range(NBLK - 1):
+                pack_copy(k).start()
+
+        for k in range(NBLK - 1):
+            tracer_copy(ch, k).start()
+        own_tracer(ch).start()
         for j in range(PER - 1):
             state_copy(ch * PER + j, dests[j]).start()
 
@@ -307,35 +339,15 @@
     own_state = pltpu.make_async_copy(snd.at[NBLK - 1], recv.at[me], self_sem)
     own_state.start()
 
-    def row(i, carry):
-        for r in range(2):
-            updf[r, pl.ds(i, 1), :] = tbuf[plan_s[r, i] // 32, r, 0:1, :]
-        return carry
-
-    lax.fori_loop(0, 32, row, 0, unroll=8)
-    usend[...] = (updf[...] + trt[...]).astype(BF16)
-
-    def tracer_copy(k):
-        return pltpu.make_async_remote_copy(
-            src_ref=usend,
-            dst_ref=trec.at[me],
-            send_sem=tssem.at[k],
-            recv_sem=trsem.at[k],
-            device_id={"lon": peers[k]},
-            device_id_type=MESH,
-        )
-
+    own_state.wait()
+    own_pack.wait()
+    for ch in range(CHUNKS):
+        own_tracer(ch).wait()
     for k in range(NBLK - 1):
-        tracer_copy(k).start()
-    own_tracer = pltpu.make_async_copy(usend, trec.at[me], tssem.at[NBLK - 1])
-    own_tracer.start()
-    own_state.wait()
-    own_plan.wait()
-    own_tracer.wait()
-    for k in range(NBLK - 1):
-        plan_copy(k).wait()
+        pack_copy(k).wait()
         state_copy(k, peers[k]).wait()
-        tracer_copy(k).wait()
+        for ch in range(CHUNKS):
+            tracer_copy(ch, k).wait()
 
 
 def place(
@@ -355,6 +367,7 @@
     tn,
     slots_v,
     slots_s,
+    loop,
     cs,
     cf,
     in_sem,
@@ -369,8 +382,9 @@
     for load in loads:
         load.start()
     plans = prec[...]
-    mine = jnp.where(plans // 32 == me, plans % 32, 0)
-    slots_v[...] = jnp.broadcast_to(jnp.max(mine, axis=2, keepdims=True), (32, 2, 128))
+    held = (plans // 32 == me) & (_iota((32, 8, 128), 2) < 32) & (_iota((32, 8, 128), 1) < 2)
+    mine = jnp.where(held, plans % 32, 0)
+    slots_v[...] = jnp.broadcast_to(jnp.max(mine, axis=2, keepdims=True), (32, 8, 128))
     to_smem = pltpu.make_async_copy(slots_v, slots_s, slot_sem)
     to_smem.start()
 
@@ -381,13 +395,20 @@
             at = (r * 6 + f) * STEP
             tend_out[r, f] = tn[at : at + 32, 0:72]
 
+    target = _iota((64, 64), 0)
+    for s in range(32):
+        spots = jnp.broadcast_to(prec[s, 2:3, 0:64], (64, 64))
+        rows = _dot(_onehot(spots == target), trec[s].reshape(64, 128))
+        for r in range(2):
+            loop[r, 32 * s : 32 * s + 32, :] = rows[32 * r : 32 * r + 32]
+
     cs[...] = jnp.zeros_like(cs)
     cf[...] = jnp.zeros_like(cf)
     cs[0:2, 0:72] = shift[...]
     cf[0:2, 0:72] = frac[...]
     for r in range(2):
         base = (me * 32 - 1 - cs[r : r + 1, :]) & 1023
-        whole = trec[:, r].astype(F32).reshape(1024, 128)
+        whole = loop[r]
         cut = jnp.concatenate([whole[512:1024], whole[0:32]], axis=0)
         now = jnp.where((base & 512) != 0, cut, whole[0:544])
         for size in (256, 128, 64, 32, 16, 8):
@@ -457,11 +478,11 @@
         advance,
         out_shape=(
             jax.ShapeDtypeStruct((32, 2, 58, 384), BF16),
-            jax.ShapeDtypeStruct((32, 2, 32, 128), BF16),
-            jax.ShapeDtypeStruct((32, 2, 32), jnp.int32),
+            jax.ShapeDtypeStruct((32, CHUNKS, 2 * PER, 128), BF16),
+            jax.ShapeDtypeStruct((32, 8, 128), jnp.int32),
             jax.ShapeDtypeStruct((32, 2, 8, 128), F32),
         ),
-        in_specs=[smem, smem, vmem, hbm] + [vmem] * 6,
+        in_specs=[smem, vmem, hbm] + [vmem] * 6,
         out_specs=(hbm, hbm, hbm, vmem),
         scratch_shapes=[
             pltpu.VMEM((2, 58, 32, 384), BF16),
@@ -480,9 +501,10 @@
             pltpu.VMEM((64, 128), F32),
             pltpu.VMEM((64, 128), F32),
             pltpu.VMEM((2, 32, 128), F32),
-            pltpu.VMEM((2, 32, 128), F32),
-            pltpu.VMEM((2, 32, 128), BF16),
+            pltpu.VMEM((2 * PER, 128), F32),
+            pltpu.VMEM((CHUNKS, 2 * PER, 128), BF16),
             pltpu.VMEM((32, 2, 58, 384), BF16),
+            pltpu.VMEM((8, 128), jnp.int32),
             pltpu.VMEM((2, 32, 128), jnp.int32),
             pltpu.SMEM((2, 32, 128), jnp.int32),
             dma((2,)),
@@ -492,13 +514,12 @@
             dma((NBLK,)),
             dma((NBLK,)),
             dma((NBLK,)),
-            dma((NBLK,)),
-            dma((NBLK,)),
+            dma((CHUNKS, NBLK)),
+            dma((CHUNKS, NBLK)),
         ],
         compiler_params=pltpu.CompilerParams(collective_id=0, has_side_effects=True),
         name="advance",
     )(
-        load_plan,
         micro_flags,
         load_plan,
         jnp.transpose(crm_state, (0, 2, 1, 3)),
@@ -523,8 +544,9 @@
             pltpu.VMEM((3, 2 * 58 * STEP, 128), F32),
             pltpu.VMEM((2, 58, 32, 384), BF16),
             pltpu.VMEM((2 * 6 * STEP, 128), F32),
-            pltpu.VMEM((32, 2, 128), jnp.int32),
-            pltpu.SMEM((32, 2, 128), jnp.int32),
+            pltpu.VMEM((32, 8, 128), jnp.int32),
+            pltpu.SMEM((32, 8, 128), jnp.int32),
+            pltpu.VMEM((2, 1024, 128), F32),
             pltpu.VMEM((8, 128), jnp.int32),
             pltpu.VMEM((8, 128), F32),
             dma((4,)),

time: 76.2 us -> 73.9 us (0.970)
  Pallas kernels: 75 us -> 72.4 us
    pallas_call x1, Pallas kernels: 69.1 us -> 64.9 us  [per_device(): pl.pallas_call(advance, out_shape=(jax.ShapeDtypeStruct((32, 2, 58, 384),...]
    pallas_call x1, Pallas kernels: 5.86 us -> 7.44 us  [per_device(): pl.pallas_call(place, out_shape=(jax.ShapeDtypeStruct((2, 58, 32, 384), B...]
where the time goes in v3:
time: 73.9 us; the launch traced here: 73 us
  Pallas kernels  72.4 us (98%)
    pallas_call x1, Pallas kernels, per_device(): pl.pallas_call(advance, out_shape=(jax.ShapeDtypeStruct((32, 2, 58, 384),...  64.9 us
    pallas_call x1, Pallas kernels, per_device(): pl.pallas_call(place, out_shape=(jax.ShapeDtypeStruct((2, 58, 32, 384), B...  7.44 us

profile of v3, /device:TPU:16, one launch (start us, length us, event | category | flops | bytes accessed | tf_op | source)
XLA Modules:
  0.0 73.0 jit_solution(555695261083862798)
XLA Ops:
  0.6 64.9 %advance.1 = (bf16[32,2,58,384]{3,2,1,0:T(8,128)(2,1)}, bf16[32,4,16,128]{3,2,1,0:T(8,128)(2,1)}, s32[32,8,128]{2,1,0:T(8,128)}, f32[32,2,8,128]{3,2,1,0:T(8,128)}) custom-call(s32[2,32]{1,0:T(2,128)} %flags.1, s32[2,32]{1,0:T(2,128)} %plan_s.1, bf16[2,58,32,384]{3,2,1,0:T(8,128)(2,1)} %bitcast.7, bf16[2,6,32,72]{3,2,1,0:T(8,128)(2,1)} %bitcast.8, ...), custom_call_target="tpu_custom_call" | custom-call | tf_op jit(solution)/shard_map/advance/pallas_call | solution.py:477
  65.6 7.4 %place.1 = (bf16[2,58,32,384]{3,2,1,0:T(8,128)(2,1)}, f32[2,6,32,72]{3,2,1,0:T(8,128)}, f32[2,32,72]{2,1,0:T(8,128)}) custom-call(s32[2,32]{1,0:T(2,128)} %plan_s.1, bf16[32,2,58,384]{3,2,1,0:T(8,128)(2,1)} %get-tuple-element.10.recv, bf16[32,4,16,128]{3,2,1,0:T(8,128)(2,1)} %get-tuple-element.11.trec, s32[32,8,128]{2,1,0:T(8,128)} %get-tuple-element.12.prec, ...), custom_call_target="tpu_custom_call" | custom-call | tf_op jit(solution)/shard_map/place/pallas_call | solution.py:533

commit v4 on v3

--- a/solution.py
+++ b/solution.py
@@ -24,6 +24,8 @@
     ((a, b, c) for a in range(4) for b in range(4) for c in range(2)),
     key=lambda off: (-_hops(off), off),
 )
+OFFSETS = OFFSETS[0:8] + OFFSETS[16:24] + OFFSETS[8:16] + OFFSETS[24:32]
+GUEST = 1
 NBLK = len(OFFSETS)
 CHUNKS = 4
 PER = NBLK // CHUNKS
@@ -97,6 +99,12 @@
     updf,
     usend,
     snd,
+    raw,
+    gsnd,
+    graw,
+    tout,
+    tsnd,
+    tback,
     pack,
     order_v,
     order,
@@ -109,6 +117,10 @@
     prsem,
     tssem,
     trsem,
+    gssem,
+    grsem,
+    bssem,
+    brsem,
 ):
     me = lax.axis_index("lon")
     loads = [pltpu.make_async_copy(crm.at[r], crm_v.at[r], in_sem.at[r]) for r in range(2)]
@@ -175,6 +187,9 @@
 
         lax.fori_loop(0, 58, widen, 0, unroll=2)
     to_smem.wait()
+    low58 = _iota((58, 128), 1) < 64
+    low64 = _iota((64, 128), 1) < 64
+    low1 = _iota((1, 128), 1) < 64
 
     def pack_copy(k):
         return pltpu.make_async_remote_copy(
@@ -202,10 +217,6 @@
     def own_tracer(ch):
         return pltpu.make_async_copy(usend.at[ch], trec.at[me, ch], tssem.at[ch, NBLK - 1])
 
-    low58 = _iota((58, 128), 1) < 64
-    low64 = _iota((64, 128), 1) < 64
-    low1 = _iota((1, 128), 1) < 64
-
     def state_copy(k, dest):
         return pltpu.make_async_remote_copy(
             src_ref=snd.at[k],
@@ -216,36 +227,123 @@
             device_id_type=MESH,
         )
 
+    guests = [GUEST * PER + p for p in range(PER)]
+    homes = [_shifted(me, [(n - d) % n for d, n in zip(OFFSETS[k], SIZES)]) for k in guests]
+
+    def raw_copy(p):
+        return pltpu.make_async_remote_copy(
+            src_ref=snd.at[guests[p]],
+            dst_ref=raw.at[p],
+            send_sem=ssem.at[guests[p]],
+            recv_sem=rsem.at[guests[p]],
+            device_id={"lon": peers[guests[p]]},
+            device_id_type=MESH,
+        )
+
+    def gcm_copy(p):
+        return pltpu.make_async_remote_copy(
+            src_ref=gsnd.at[p],
+            dst_ref=graw.at[p],
+            send_sem=gssem.at[p],
+            recv_sem=grsem.at[p],
+            device_id={"lon": peers[guests[p]]},
+            device_id_type=MESH,
+        )
+
+    def back_copy(p):
+        return pltpu.make_async_remote_copy(
+            src_ref=tsnd.at[p],
+            dst_ref=tback.at[p],
+            send_sem=bssem.at[p],
+            recv_sem=brsem.at[p],
+            device_id={"lon": homes[p]},
+            device_id_type=MESH,
+        )
+
+    def guest_copy(p):
+        return pltpu.make_async_copy(snd.at[guests[p]], recv.at[homes[p]], self_sem.at[p])
+
+    def fetch(r, i):
+        column = [cn[t, pl.ds(r * 58 * STEP + i, 58, stride=STEP), :] for t in range(3)]
+        flag = jnp.where(flags[r, i] == 1, jnp.float32(1), jnp.float32(0))
+        return column, gn[pl.ds(r * 6 * STEP + i, 6, stride=STEP), :], jnp.full((1, 128), flag)
+
+    gsnd[...] = jnp.zeros_like(gsnd)
+    for p in range(PER):
+        for r in range(2):
+            column, model, flag = fetch(r, order[r, peers[guests[p]], 0])
+            for t in range(3):
+                snd[guests[p], r, :, 128 * t : 128 * t + 128] = column[t].astype(BF16)
+            gsnd[p, 8 * r : 8 * r + 6, :] = model
+            gsnd[p, 8 * r + 6 : 8 * r + 7, :] = flag
+    pl.semaphore_wait(barrier, NBLK - 1)
+    for p in range(PER):
+        raw_copy(p).start()
+        gcm_copy(p).start()
+    for k in range(NBLK - 1):
+        pack_copy(k).start()
+
+    def enter(p, one, two):
+        first = jnp.where(low58, one[0], pltpu.roll(two[0], 64, 1))
+        second = jnp.where(low58, pltpu.roll(one[0], 64, 1), two[0])
+        s0[p, 0:58, 0:128] = first
+        s0[p, 0:58, 128:256] = second
+        blocks = ((first, second), (one[1], two[1]), (one[2], two[2]))
+        for t in range(3):
+            for half in range(2):
+                narrow = blocks[t][half].astype(BF16)
+                xs[t * PER + p, 0:58, 128 * half : 128 * half + 128] = narrow
+                x0[t * PER + p, 0:58, 128 * half : 128 * half + 128] = narrow
+
+    def tell(ch, places, rows):
+        for p in range(PER):
+            for r in range(2):
+                home = pl.ds(order[r, places[p], 0], 1)
+                tbuf[places[p], r] = rows[p, r]
+                updf[2 * p + r : 2 * p + r + 1, :] = rows[p, r, 0:1, :] + trt[r, home, :]
+        usend[ch] = updf[...].astype(BF16)
+        for k in range(NBLK - 1):
+            tracer_copy(ch, k).start()
+        own_tracer(ch).start()
+
     def chunk(ch, carry):
         dests = []
         for j in range(PER):
             offs = [OFFSETS[c * PER + j] for c in range(CHUNKS)]
             off = [_pick(ch, [o[i] for o in offs]) for i in range(3)]
             dests.append(_shifted(me, off))
+
+        @pl.when(ch != GUEST)
+        def _():
+            for p in range(PER):
+                pair = []
+                for r in range(2):
+                    column, model, flag = fetch(r, order[r, dests[p], 0])
+                    row = 16 * p + 8 * r
+                    gsc[row : row + 6, :] = model
+                    gsc[row + 6 : row + 7, :] = flag
+                    pair.append(column)
+                enter(p, *pair)
+
+        @pl.when(ch == GUEST)
+        def _():
+            for p in range(PER):
+                raw_copy(p).wait()
+                gcm_copy(p).wait()
+            for p in range(PER):
+                pair = []
+                for r in range(2):
+                    column = raw[p, r].astype(F32)
+                    pair.append([column[:, 128 * t : 128 * t + 128] for t in range(3)])
+                gsc[16 * p : 16 * p + 16, :] = graw[p]
+                enter(p, *pair)
+
         avs, bvs = [], []
         for p in range(PER):
-            cols, a, b = [], [], []
-            for r in range(2):
-                i = order[r, dests[p], 0]
-                cols.append([cn[t, pl.ds(r * 58 * STEP + i, 58, stride=STEP), :] for t in range(3)])
-                row = 16 * p + 8 * r
-                gsc[row : row + 6, :] = gn[pl.ds(r * 6 * STEP + i, 6, stride=STEP), :]
-                flag = flags[r, i]
-                a.append(jnp.where(flag == 1, jnp.float32(0.5), jnp.float32(0)))
-                b.append(jnp.where(flag == 1, jnp.float32(0), jnp.float32(-0.25)))
-            avs.append(jnp.where(low1, a[0], a[1]))
-            bvs.append(jnp.where(low1, b[0], b[1]))
-            one, two = cols[0][0], cols[1][0]
-            first = jnp.where(low58, one, pltpu.roll(two, 64, 1))
-            second = jnp.where(low58, pltpu.roll(one, 64, 1), two)
-            s0[p, 0:58, 0:128] = first
-            s0[p, 0:58, 128:256] = second
-            blocks = ((first, second), (cols[0][1], cols[1][1]), (cols[0][2], cols[1][2]))
-            for t in range(3):
-                for half in range(2):
-                    narrow = blocks[t][half].astype(BF16)
-                    xs[t * PER + p, 0:58, 128 * half : 128 * half + 128] = narrow
-                    x0[t * PER + p, 0:58, 128 * half : 128 * half + 128] = narrow
+            row = 16 * p + 6
+            flag = jnp.where(low1, gsc[row : row + 1, :], gsc[row + 8 : row + 9, :])
+            avs.append(0.5 * flag)
+            bvs.append(0.25 * flag - 0.25)
         forcing = lax.dot_general(
             tc[...],
             gsc[...],
@@ -298,10 +396,7 @@
         for p in range(PER):
             for r in range(2):
                 row = 16 * p + 8 * r
-                tbuf[dests[p], r] = tend[row : row + 8]
-                home = pl.ds(order[r, dests[p], 0], 1)
-                updf[2 * p + r : 2 * p + r + 1, :] = tend[row : row + 1] + trt[r, home, :]
-        usend[ch] = updf[...].astype(BF16)
+                tout[p, r] = tend[row : row + 8]
 
         for p in range(PER):
             k = ch * PER + p
@@ -316,36 +411,46 @@
                         t * PER + p, 0:58, 128 * r : 128 * r + 128
                     ]
 
-        @pl.when(ch == 0)
+        @pl.when(ch != GUEST)
         def _():
-            pl.semaphore_wait(barrier, NBLK - 1)
-            for k in range(NBLK - 1):
-                pack_copy(k).start()
-
-        for k in range(NBLK - 1):
-            tracer_copy(ch, k).start()
-        own_tracer(ch).start()
-        for j in range(PER - 1):
-            state_copy(ch * PER + j, dests[j]).start()
-
-        @pl.when(ch < CHUNKS - 1)
+            tell(ch, dests, tout)
+            for j in range(PER - 1):
+                state_copy(ch * PER + j, dests[j]).start()
+
+        @pl.when((ch != GUEST) & (ch < CHUNKS - 1))
         def _():
             state_copy(ch * PER + PER - 1, dests[PER - 1]).start()
 
+        @pl.when(ch == GUEST)
+        def _():
+            tsnd[...] = tout[...]
+            for p in range(PER):
+                back_copy(p).start()
+                guest_copy(p).start()
+
+        @pl.when(ch == GUEST + 1)
+        def _():
+            for p in range(PER):
+                back_copy(p).wait()
+            tell(GUEST, [peers[k] for k in guests], tback)
+
         return carry
 
     lax.fori_loop(0, CHUNKS, chunk, 0)
 
-    own_state = pltpu.make_async_copy(snd.at[NBLK - 1], recv.at[me], self_sem)
+    own_state = pltpu.make_async_copy(snd.at[NBLK - 1], recv.at[me], self_sem.at[PER])
     own_state.start()
 
     own_state.wait()
     own_pack.wait()
     for ch in range(CHUNKS):
         own_tracer(ch).wait()
+    for p in range(PER):
+        guest_copy(p).wait()
     for k in range(NBLK - 1):
         pack_copy(k).wait()
-        state_copy(k, peers[k]).wait()
+        if k not in guests:
+            state_copy(k, peers[k]).wait()
         for ch in range(CHUNKS):
             tracer_copy(ch, k).wait()
 
@@ -504,18 +609,28 @@
             pltpu.VMEM((2 * PER, 128), F32),
             pltpu.VMEM((CHUNKS, 2 * PER, 128), BF16),
             pltpu.VMEM((32, 2, 58, 384), BF16),
+            pltpu.VMEM((PER, 2, 58, 384), BF16),
+            pltpu.VMEM((PER, 16, 128), F32),
+            pltpu.VMEM((PER, 16, 128), F32),
+            pltpu.VMEM((PER, 2, 8, 128), F32),
+            pltpu.VMEM((PER, 2, 8, 128), F32),
+            pltpu.VMEM((PER, 2, 8, 128), F32),
             pltpu.VMEM((8, 128), jnp.int32),
             pltpu.VMEM((2, 32, 128), jnp.int32),
             pltpu.SMEM((2, 32, 128), jnp.int32),
             dma((2,)),
             dma,
-            dma,
+            dma((PER + 1,)),
             dma((NBLK,)),
             dma((NBLK,)),
             dma((NBLK,)),
             dma((NBLK,)),
             dma((CHUNKS, NBLK)),
             dma((CHUNKS, NBLK)),
+            dma((PER,)),
+            dma((PER,)),
+            dma((PER,)),
+            dma((PER,)),
         ],
         compiler_params=pltpu.CompilerParams(collective_id=0, has_side_effects=True),
         name="advance",

time: 73.9 us -> 90.4 us (1.22)
  Pallas kernels: 72.4 us -> 89.4 us
    pallas_call x1, Pallas kernels: 64.9 us -> 82 us  [per_device(): pl.pallas_call(advance, out_shape=(jax.ShapeDtypeStruct((32, 2, 58, 384),...]
where the time goes in v4:
time: 90.4 us; the launch traced here: 90.2 us
  Pallas kernels  89.4 us (99%)
    pallas_call x1, Pallas kernels, per_device(): pl.pallas_call(advance, out_shape=(jax.ShapeDtypeStruct((32, 2, 58, 384),...  82 us
    pallas_call x1, Pallas kernels, per_device(): pl.pallas_call(place, out_shape=(jax.ShapeDtypeStruct((2, 58, 32, 384), B...  7.44 us

profile of v4, /device:TPU:16, one launch (start us, length us, event | category | flops | bytes accessed | tf_op | source)
XLA Modules:
  0.0 90.2 jit_solution(16675012779831620572)
XLA Ops:
  0.6 82.0 %advance.1 = (bf16[32,2,58,384]{3,2,1,0:T(8,128)(2,1)}, bf16[32,4,16,128]{3,2,1,0:T(8,128)(2,1)}, s32[32,8,128]{2,1,0:T(8,128)}, f32[32,2,8,128]{3,2,1,0:T(8,128)}) custom-call(s32[2,32]{1,0:T(2,128)} %flags.1, s32[2,32]{1,0:T(2,128)} %plan_s.1, bf16[2,58,32,384]{3,2,1,0:T(8,128)(2,1)} %bitcast.7, bf16[2,6,32,72]{3,2,1,0:T(8,128)(2,1)} %bitcast.8, ...), custom_call_target="tpu_custom_call" | custom-call | tf_op jit(solution)/shard_map/advance/pallas_call | solution.py:582
  82.6 7.4 %place.1 = (bf16[2,58,32,384]{3,2,1,0:T(8,128)(2,1)}, f32[2,6,32,72]{3,2,1,0:T(8,128)}, f32[2,32,72]{2,1,0:T(8,128)}) custom-call(s32[2,32]{1,0:T(2,128)} %plan_s.1, bf16[32,2,58,384]{3,2,1,0:T(8,128)(2,1)} %get-tuple-element.10.recv, bf16[32,4,16,128]{3,2,1,0:T(8,128)(2,1)} %get-tuple-element.11.trec, s32[32,8,128]{2,1,0:T(8,128)} %get-tuple-element.12.prec, ...), custom_call_target="tpu_custom_call" | custom-call | tf_op jit(solution)/shard_map/place/pallas_call | solution.py:648

commit v5 on v3

--- a/solution.py
+++ b/solution.py
@@ -55,6 +55,10 @@
 
 def _onehot(mask):
     return jnp.where(mask, jnp.float32(1), jnp.float32(0)).astype(BF16)
+
+
+def _part(r, t):
+    return slice(58 * (3 * r + t), 58 * (3 * r + t) + 58)
 
 
 def _lane_map(quarter, lanes):
@@ -77,6 +81,7 @@
     recv,
     trec,
     prec,
+    tend_out,
     tbuf,
     crm_v,
     cn,
@@ -103,6 +108,7 @@
     in_sem,
     order_sem,
     self_sem,
+    tend_sem,
     ssem,
     rsem,
     pssem,
@@ -308,13 +314,11 @@
             one, two = s0[p, :, 0:128], s0[p, :, 128:256]
             left = jnp.where(low64, one, pltpu.roll(two, 64, 1)).astype(BF16)
             right = jnp.where(low64, pltpu.roll(one, 64, 1), two).astype(BF16)
-            snd[k, 0, :, 0:128] = left[0:58]
-            snd[k, 1, :, 0:128] = right[0:58]
+            snd[k, _part(0, 0), :] = left[0:58]
+            snd[k, _part(1, 0), :] = right[0:58]
             for t in (1, 2):
                 for r in range(2):
-                    snd[k, r, :, 128 * t : 128 * t + 128] = xs[
-                        t * PER + p, 0:58, 128 * r : 128 * r + 128
-                    ]
+                    snd[k, _part(r, t), :] = xs[t * PER + p, 0:58, 128 * r : 128 * r + 128]
 
         @pl.when(ch == 0)
         def _():
@@ -338,7 +342,10 @@
 
     own_state = pltpu.make_async_copy(snd.at[NBLK - 1], recv.at[me], self_sem)
     own_state.start()
-
+    tend_copy = pltpu.make_async_copy(tbuf, tend_out, tend_sem)
+    tend_copy.start()
+
+    tend_copy.wait()
     own_state.wait()
     own_pack.wait()
     for ch in range(CHUNKS):
@@ -353,14 +360,19 @@
 def place(
     plan_s,
     recv,
-    trec,
-    prec,
-    tbuf,
+    trec_hbm,
+    prec_hbm,
+    tbuf_hbm,
     shift,
     frac,
     state_out,
     tend_out,
     polar_out,
+    prec,
+    tbuf,
+    trec,
+    tend_v,
+    polar_v,
     rbuf,
     wide,
     obuf,
@@ -370,31 +382,41 @@
     loop,
     cs,
     cf,
+    small_sem,
     in_sem,
     slot_sem,
     out_sem,
 ):
     me = lax.axis_index("lon")
+    smalls = [
+        pltpu.make_async_copy(src, dst, small_sem.at[n])
+        for n, (src, dst) in enumerate(((prec_hbm, prec), (tbuf_hbm, tbuf), (trec_hbm, trec)))
+    ]
     loads = [
         pltpu.make_async_copy(recv.at[pl.ds(8 * q, 8)], rbuf.at[pl.ds(8 * q, 8)], in_sem.at[q])
         for q in range(4)
     ]
-    for load in loads:
+    for load in smalls + loads:
         load.start()
+    smalls[0].wait()
     plans = prec[...]
     held = (plans // 32 == me) & (_iota((32, 8, 128), 2) < 32) & (_iota((32, 8, 128), 1) < 2)
     mine = jnp.where(held, plans % 32, 0)
     slots_v[...] = jnp.broadcast_to(jnp.max(mine, axis=2, keepdims=True), (32, 8, 128))
     to_smem = pltpu.make_async_copy(slots_v, slots_s, slot_sem)
     to_smem.start()
+    smalls[1].wait()
 
     for r in range(2):
         for i in range(32):
             tn[pl.ds(r * 6 * STEP + i, 6, stride=STEP), :] = tbuf[plan_s[r, i] // 32, r, 0:6, :]
         for f in range(6):
             at = (r * 6 + f) * STEP
-            tend_out[r, f] = tn[at : at + 32, 0:72]
-
+            tend_v[r, f] = tn[at : at + 32, 0:72]
+    outs = [pltpu.make_async_copy(tend_v, tend_out, out_sem.at[4])]
+    outs[0].start()
+
+    smalls[2].wait()
     target = _iota((64, 64), 0)
     for s in range(32):
         spots = jnp.broadcast_to(prec[s, 2:3, 0:64], (64, 64))
@@ -418,7 +440,9 @@
             now = jnp.where((base & size) != 0, pltpu.roll(now, 40 - size, 0), now)
         weight = cf[r : r + 1, :]
         result = (1.0 - weight) * pltpu.roll(now, 39, 0) + weight * now
-        polar_out[r] = result[0:32, 0:72]
+        polar_v[r] = result[0:32, 0:72]
+    outs.append(pltpu.make_async_copy(polar_v, polar_out, out_sem.at[5]))
+    outs[1].start()
 
     to_smem.wait()
     for q in range(4):
@@ -426,15 +450,13 @@
 
         def spot(s, carry):
             for r in range(2):
-                column = rbuf[s, r].astype(F32)
                 at = pl.ds(r * 58 * STEP + slots_s[s, r, 0], 58, stride=STEP)
                 for t in range(3):
-                    wide[t, at, :] = column[:, 128 * t : 128 * t + 128]
+                    wide[t, at, :] = rbuf[s, _part(r, t), :].astype(F32)
             return carry
 
         lax.fori_loop(8 * q, 8 * q + 8, spot, 0, unroll=2)
 
-    outs = []
     for r in range(2):
         for part in range(2):
 
@@ -477,14 +499,15 @@
     recv, trec, prec, tbuf = pl.pallas_call(
         advance,
         out_shape=(
-            jax.ShapeDtypeStruct((32, 2, 58, 384), BF16),
+            jax.ShapeDtypeStruct((32, 348, 128), BF16),
             jax.ShapeDtypeStruct((32, CHUNKS, 2 * PER, 128), BF16),
             jax.ShapeDtypeStruct((32, 8, 128), jnp.int32),
             jax.ShapeDtypeStruct((32, 2, 8, 128), F32),
         ),
         in_specs=[smem, vmem, hbm] + [vmem] * 6,
-        out_specs=(hbm, hbm, hbm, vmem),
+        out_specs=(hbm, hbm, hbm, hbm),
         scratch_shapes=[
+            pltpu.VMEM((32, 2, 8, 128), F32),
             pltpu.VMEM((2, 58, 32, 384), BF16),
             pltpu.VMEM((3, 2 * 58 * STEP, 128), F32),
             pltpu.VMEM((3 * PER, 64, 256), BF16),
@@ -503,11 +526,12 @@
             pltpu.VMEM((2, 32, 128), F32),
             pltpu.VMEM((2 * PER, 128), F32),
             pltpu.VMEM((CHUNKS, 2 * PER, 128), BF16),
-            pltpu.VMEM((32, 2, 58, 384), BF16),
+            pltpu.VMEM((32, 348, 128), BF16),
             pltpu.VMEM((8, 128), jnp.int32),
             pltpu.VMEM((2, 32, 128), jnp.int32),
             pltpu.SMEM((2, 32, 128), jnp.int32),
             dma((2,)),
+            dma,
             dma,
             dma,
             dma((NBLK,)),
@@ -537,10 +561,15 @@
             jax.ShapeDtypeStruct((2, 6, 32, 72), F32),
             jax.ShapeDtypeStruct((2, 32, 72), F32),
         ),
-        in_specs=[smem, hbm] + [vmem] * 5,
-        out_specs=(hbm, vmem, vmem),
+        in_specs=[smem] + [hbm] * 4 + [vmem] * 2,
+        out_specs=(hbm, hbm, hbm),
         scratch_shapes=[
-            pltpu.VMEM((32, 2, 58, 384), BF16),
+            pltpu.VMEM((32, 8, 128), jnp.int32),
+            pltpu.VMEM((32, 2, 8, 128), F32),
+            pltpu.VMEM((32, CHUNKS, 2 * PER, 128), BF16),
+            pltpu.VMEM((2, 6, 32, 72), F32),
+            pltpu.VMEM((2, 32, 72), F32),
+            pltpu.VMEM((32, 348, 128), BF16),
             pltpu.VMEM((3, 2 * 58 * STEP, 128), F32),
             pltpu.VMEM((2, 58, 32, 384), BF16),
             pltpu.VMEM((2 * 6 * STEP, 128), F32),
@@ -549,9 +578,10 @@
             pltpu.VMEM((2, 1024, 128), F32),
             pltpu.VMEM((8, 128), jnp.int32),
             pltpu.VMEM((8, 128), F32),
+            dma((3,)),
             dma((4,)),
             dma,
-            dma((4,)),
+            dma((6,)),
         ],
         name="place",
     )(load_plan, recv, trec, prec, tbuf, courant_shift, courant_frac)

time: 73.9 us -> 69.3 us (0.938)
  Pallas kernels: 72.4 us -> 68.1 us
    pallas_call x1, Pallas kernels: 64.9 us -> 60.9 us  [per_device(): pl.pallas_call(advance, out_shape=(jax.ShapeDtypeStruct((32, 348, 128), B...]
where the time goes in v5:
time: 69.3 us; the launch traced here: 68.7 us
  Pallas kernels  68.1 us (98%)
    pallas_call x1, Pallas kernels, per_device(): pl.pallas_call(advance, out_shape=(jax.ShapeDtypeStruct((32, 348, 128), B...  60.9 us
    pallas_call x1, Pallas kernels, per_device(): pl.pallas_call(place, out_shape=(jax.ShapeDtypeStruct((2, 58, 32, 384), B...  7.14 us

profile of v5, /device:TPU:16, one launch (start us, length us, event | category | flops | bytes accessed | tf_op | source)
XLA Modules:
  0.0 68.7 jit_solution(18151376176945191845)
XLA Ops:
  0.6 60.9 %advance.1 = (bf16[32,348,128]{2,1,0:T(8,128)(2,1)}, bf16[32,4,16,128]{3,2,1,0:T(8,128)(2,1)}, s32[32,8,128]{2,1,0:T(8,128)}, f32[32,2,8,128]{3,2,1,0:T(8,128)}) custom-call(s32[2,32]{1,0:T(2,128)} %flags.1, s32[2,32]{1,0:T(2,128)} %plan_s.1, bf16[2,58,32,384]{3,2,1,0:T(8,128)(2,1)} %bitcast.7, bf16[2,6,32,72]{3,2,1,0:T(8,128)(2,1)} %bitcast.8, ...), custom_call_target="tpu_custom_call" | custom-call | tf_op jit(solution)/shard_map/advance/pallas_call | solution.py:499
  61.6 7.1 %place.1 = (bf16[2,58,32,384]{3,2,1,0:T(8,128)(2,1)}, f32[2,6,32,72]{3,2,1,0:T(8,128)}, f32[2,32,72]{2,1,0:T(8,128)}) custom-call(s32[2,32]{1,0:T(2,128)} %plan_s.1, bf16[32,348,128]{2,1,0:T(8,128)(2,1)} %get-tuple-element.10.recv, bf16[32,4,16,128]{3,2,1,0:T(8,128)(2,1)} %get-tuple-element.11.trec_hbm, s32[32,8,128]{2,1,0:T(8,128)} %get-tuple-element.12.prec_hbm, ...), custom_call_target="tpu_custom_call" | custom-call | tf_op jit(solution)/shard_map/place/pallas_call | solution.py:557

commit v6 on v5

--- a/solution.py
+++ b/solution.py
@@ -24,6 +24,8 @@
     ((a, b, c) for a in range(4) for b in range(4) for c in range(2)),
     key=lambda off: (-_hops(off), off),
 )
+NEAR = [(1, 1, 0), (3, 3, 0), (1, 0, 0), (3, 0, 0), (0, 1, 0), (0, 3, 0), (0, 0, 1), (0, 0, 0)]
+OFFSETS = [off for off in OFFSETS if off not in NEAR] + NEAR
 NBLK = len(OFFSETS)
 CHUNKS = 4
 PER = NBLK // CHUNKS
@@ -83,7 +85,6 @@
     prec,
     tend_out,
     tbuf,
-    crm_v,
     cn,
     xs,
     x0,
@@ -105,7 +106,6 @@
     pack,
     order_v,
     order,
-    in_sem,
     order_sem,
     self_sem,
     tend_sem,
@@ -117,9 +117,6 @@
     trsem,
 ):
     me = lax.axis_index("lon")
-    loads = [pltpu.make_async_copy(crm.at[r], crm_v.at[r], in_sem.at[r]) for r in range(2)]
-    for load in loads:
-        load.start()
 
     peers = [_shifted(me, off) for off in OFFSETS]
     barrier = pltpu.get_barrier_semaphore()
@@ -171,10 +168,9 @@
             gn[(r * 6 + f) * STEP : (r * 6 + f) * STEP + 32, 0:72] = gcm[r, f].astype(F32)
 
     for r in range(2):
-        loads[r].wait()
 
         def widen(level, carry):
-            block = crm_v[r, level].astype(F32)
+            block = crm[r, level].astype(F32)
             for t in range(3):
                 cn[t, pl.ds((r * 58 + level) * STEP, 32), :] = block[:, 128 * t : 128 * t + 128]
             return carry
@@ -360,20 +356,16 @@
 def place(
     plan_s,
     recv,
-    trec_hbm,
-    prec_hbm,
-    tbuf_hbm,
+    trec,
+    prec,
+    tbuf,
     shift,
     frac,
     state_out,
     tend_out,
     polar_out,
-    prec,
-    tbuf,
-    trec,
     tend_v,
     polar_v,
-    rbuf,
     wide,
     obuf,
     tn,
@@ -382,30 +374,16 @@
     loop,
     cs,
     cf,
-    small_sem,
-    in_sem,
     slot_sem,
     out_sem,
 ):
     me = lax.axis_index("lon")
-    smalls = [
-        pltpu.make_async_copy(src, dst, small_sem.at[n])
-        for n, (src, dst) in enumerate(((prec_hbm, prec), (tbuf_hbm, tbuf), (trec_hbm, trec)))
-    ]
-    loads = [
-        pltpu.make_async_copy(recv.at[pl.ds(8 * q, 8)], rbuf.at[pl.ds(8 * q, 8)], in_sem.at[q])
-        for q in range(4)
-    ]
-    for load in smalls + loads:
-        load.start()
-    smalls[0].wait()
     plans = prec[...]
     held = (plans // 32 == me) & (_iota((32, 8, 128), 2) < 32) & (_iota((32, 8, 128), 1) < 2)
     mine = jnp.where(held, plans % 32, 0)
     slots_v[...] = jnp.broadcast_to(jnp.max(mine, axis=2, keepdims=True), (32, 8, 128))
     to_smem = pltpu.make_async_copy(slots_v, slots_s, slot_sem)
     to_smem.start()
-    smalls[1].wait()
 
     for r in range(2):
         for i in range(32):
@@ -416,7 +394,6 @@
     outs = [pltpu.make_async_copy(tend_v, tend_out, out_sem.at[4])]
     outs[0].start()
 
-    smalls[2].wait()
     target = _iota((64, 64), 0)
     for s in range(32):
         spots = jnp.broadcast_to(prec[s, 2:3, 0:64], (64, 64))
@@ -446,13 +423,12 @@
 
     to_smem.wait()
     for q in range(4):
-        loads[q].wait()
 
         def spot(s, carry):
             for r in range(2):
                 at = pl.ds(r * 58 * STEP + slots_s[s, r, 0], 58, stride=STEP)
                 for t in range(3):
-                    wide[t, at, :] = rbuf[s, _part(r, t), :].astype(F32)
+                    wide[t, at, :] = recv[s, _part(r, t), :].astype(F32)
             return carry
 
         lax.fori_loop(8 * q, 8 * q + 8, spot, 0, unroll=2)
@@ -504,11 +480,10 @@
             jax.ShapeDtypeStruct((32, 8, 128), jnp.int32),
             jax.ShapeDtypeStruct((32, 2, 8, 128), F32),
         ),
-        in_specs=[smem, vmem, hbm] + [vmem] * 6,
+        in_specs=[smem] + [vmem] * 8,
         out_specs=(hbm, hbm, hbm, hbm),
         scratch_shapes=[
             pltpu.VMEM((32, 2, 8, 128), F32),
-            pltpu.VMEM((2, 58, 32, 384), BF16),
             pltpu.VMEM((3, 2 * 58 * STEP, 128), F32),
             pltpu.VMEM((3 * PER, 64, 256), BF16),
             pltpu.VMEM((3 * PER, 64, 256), BF16),
@@ -530,7 +505,6 @@
             pltpu.VMEM((8, 128), jnp.int32),
             pltpu.VMEM((2, 32, 128), jnp.int32),
             pltpu.SMEM((2, 32, 128), jnp.int32),
-            dma((2,)),
             dma,
             dma,
             dma,
@@ -541,7 +515,9 @@
             dma((CHUNKS, NBLK)),
             dma((CHUNKS, NBLK)),
         ],
-        compiler_params=pltpu.CompilerParams(collective_id=0, has_side_effects=True),
+        compiler_params=pltpu.CompilerParams(
+            collective_id=0, has_side_effects=True, vmem_limit_bytes=26 << 20
+        ),
         name="advance",
     )(
         micro_flags,
@@ -561,15 +537,11 @@
             jax.ShapeDtypeStruct((2, 6, 32, 72), F32),
             jax.ShapeDtypeStruct((2, 32, 72), F32),
         ),
-        in_specs=[smem] + [hbm] * 4 + [vmem] * 2,
+        in_specs=[smem] + [vmem] * 6,
         out_specs=(hbm, hbm, hbm),
         scratch_shapes=[
-            pltpu.VMEM((32, 8, 128), jnp.int32),
-            pltpu.VMEM((32, 2, 8, 128), F32),
-            pltpu.VMEM((32, CHUNKS, 2 * PER, 128), BF16),
             pltpu.VMEM((2, 6, 32, 72), F32),
             pltpu.VMEM((2, 32, 72), F32),
-            pltpu.VMEM((32, 348, 128), BF16),
             pltpu.VMEM((3, 2 * 58 * STEP, 128), F32),
             pltpu.VMEM((2, 58, 32, 384), BF16),
             pltpu.VMEM((2 * 6 * STEP, 128), F32),
@@ -578,11 +550,10 @@
             pltpu.VMEM((2, 1024, 128), F32),
             pltpu.VMEM((8, 128), jnp.int32),
             pltpu.VMEM((8, 128), F32),
-            dma((3,)),
-            dma((4,)),
             dma,
             dma((6,)),
         ],
+        compiler_params=pltpu.CompilerParams(vmem_limit_bytes=24 << 20),
         name="place",
     )(load_plan, recv, trec, prec, tbuf, courant_shift, courant_frac)
     return (

time: 69.3 us -> 75.4 us (1.088)
  local copies, waits for them, and re-layouts: 0 us -> 7.77 us
  Pallas kernels: 68.1 us -> 66.1 us
    unnamed x0 -> x22, local copies, waits for them, and re-layouts: none -> 7.77 us
    pallas_call x1, Pallas kernels: 60.9 us -> 59.9 us  [per_device(): pl.pallas_call(advance, out_shape=(jax.ShapeDtypeStruct((32, 348, 128), B...]
    pallas_call x1, Pallas kernels: 7.14 us -> 6.18 us  [per_device(): pl.pallas_call(place, out_shape=(jax.ShapeDtypeStruct((2, 58, 32, 384), B...]
where the time goes in v6:
time: 75.4 us; the launch traced here: 74.5 us
  Pallas kernels  66.1 us (88%)
  local copies, waits for them, and re-layouts  7.77 us (10%)
    pallas_call x1, Pallas kernels, per_device(): pl.pallas_call(advance, out_shape=(jax.ShapeDtypeStruct((32, 348, 128), B...  59.9 us
    unnamed x22, local copies, waits for them, and re-layouts  7.77 us
    pallas_call x1, Pallas kernels, per_device(): pl.pallas_call(place, out_shape=(jax.ShapeDtypeStruct((2, 58, 32, 384), B...  6.18 us

profile of v6, /device:TPU:16, one launch (start us, length us, event | category | flops | bytes accessed | tf_op | source)
XLA Modules:
  0.0 74.5 jit_solution(6189163065787739050)
XLA Ops:
  0.6 0.0 copy-start.10
  0.6 0.0 copy-start.9
  0.7 0.0 copy-start
  0.7 1.8 %copy-done = bf16[2,32,58,384]{3,1,2,0:T(8,128)(2,1)S(1)} copy-done((bf16[2,32,58,384]{3,1,2,0:T(8,128)(2,1)S(1)}, bf16[2,32,58,384]{3,1,2,0:T(8,128)(2,1)}, u32[]{:S(2)}) %copy-start) | copy-done | bytes 2850840
  2.5 0.0 copy-start.1
  2.5 0.9 %copy-done.1 = bf16[2,32,6,72]{3,1,2,0:T(8,128)(2,1)S(1)} copy-done((bf16[2,32,6,72]{3,1,2,0:T(8,128)(2,1)S(1)}, bf16[2,32,6,72]{3,1,2,0:T(8,128)(2,1)}, u32[]{:S(2)}) %copy-start.1) | copy-done | bytes 55320
  3.4 0.0 copy-start.2
  3.4 0.8 %copy-done.2 = f32[58,72]{1,0:T(8,128)S(1)} copy-done((f32[58,72]{1,0:T(8,128)S(1)}, f32[58,72]{1,0:T(8,128)}, u32[]{:S(2)}) %copy-start.2) | copy-done | bytes 16728
  4.1 0.0 copy-start.3
  4.1 0.8 %copy-done.3 = f32[72,58]{0,1:T(8,128)S(1)} copy-done((f32[72,58]{0,1:T(8,128)S(1)}, f32[72,58]{0,1:T(8,128)}, u32[]{:S(2)}) %copy-start.3) | copy-done | bytes 16728
  4.9 0.0 copy-start.4
  4.9 0.8 %copy-done.4 = f32[2,72,32]{1,2,0:T(8,128)S(1)} copy-done((f32[2,72,32]{1,2,0:T(8,128)S(1)}, f32[2,72,32]{1,2,0:T(8,128)}, u32[]{:S(2)}) %copy-start.4) | copy-done | bytes 18456
  5.6 0.0 copy-start.5
  5.6 0.7 copy-done.5
  6.4 0.0 copy-start.6
  6.4 0.7 copy-done.6
  7.1 0.0 copy-start.7
  7.1 0.7 copy-done.7
  7.8 0.0 copy-start.8
  7.8 0.7 copy-done.8
  8.4 59.9 %advance.1 = (bf16[32,348,128]{2,1,0:T(8,128)(2,1)S(1)}, bf16[32,4,16,128]{3,2,1,0:T(8,128)(2,1)S(1)}, s32[32,8,128]{2,1,0:T(8,128)S(1)}, f32[32,2,8,128]{3,2,1,0:T(8,128)S(1)}) custom-call(s32[2,32]{1,0:T(2,128)S(1)} %copy-done.8, s32[2,32]{1,0:T(2,128)S(1)} %copy-done.7, bf16[2,58,32,384]{3,2,1,0:T(8,128)(2,1)S(1)} %bitcast.7, ...), custom_call_target="tpu_custom_call" | custom-call | tf_op jit(solution)/shard_map/advance/pallas_call | solution.py:475
  68.3 0.0 copy-done.10
  68.3 0.0 copy-done.9
  68.4 6.2 %place.1 = (bf16[2,58,32,384]{3,2,1,0:T(8,128)(2,1)}, f32[2,6,32,72]{3,2,1,0:T(8,128)}, f32[2,32,72]{2,1,0:T(8,128)}) custom-call(s32[2,32]{1,0:T(2,128)S(1)} %copy-done.7, bf16[32,348,128]{2,1,0:T(8,128)(2,1)S(1)} %get-tuple-element.10.recv, bf16[32,4,16,128]{3,2,1,0:T(8,128)(2,1)S(1)} %get-tuple-element.11.trec, s32[32,8,128]{2,1,0:T(8,128)S(1)} %get-tuple-element.12.prec, ...), custom_call_target="tpu_custom_call" | custom-call | tf_op jit(solution)/shard_map/place/pallas_call | solution.py:533
Async XLA Ops:
  0.6 67.7 %copy-start.10 = (f32[2,72]{1,0:T(2,128)S(1)}, f32[2,72]{1,0:T(2,128)}, u32[]{:S(2)}) copy-start(f32[2,72]{1,0:T(2,128)} %frac.1) | copy-start | bytes 1732
  0.6 67.7 %copy-start.9 = (s32[2,72]{1,0:T(2,128)S(1)}, s32[2,72]{1,0:T(2,128)}, u32[]{:S(2)}) copy-start(s32[2,72]{1,0:T(2,128)} %shift.1) | copy-start | bytes 1732
  0.7 1.8 %copy-start = (bf16[2,32,58,384]{3,1,2,0:T(8,128)(2,1)S(1)}, bf16[2,32,58,384]{3,1,2,0:T(8,128)(2,1)}, u32[]{:S(2)}) copy-start(bf16[2,32,58,384]{3,1,2,0:T(8,128)(2,1)} %param.11) | copy-start | bytes 8552452
  2.5 0.9 %copy-start.1 = (bf16[2,32,6,72]{3,1,2,0:T(8,128)(2,1)S(1)}, bf16[2,32,6,72]{3,1,2,0:T(8,128)(2,1)}, u32[]{:S(2)}) copy-start(bf16[2,32,6,72]{3,1,2,0:T(8,128)(2,1)} %param.12) | copy-start | bytes 165892
  3.4 0.8 %copy-start.2 = (f32[58,72]{1,0:T(8,128)S(1)}, f32[58,72]{1,0:T(8,128)}, u32[]{:S(2)}) copy-start(f32[58,72]{1,0:T(8,128)} %to_crm.1) | copy-start | bytes 50116
  4.1 0.8 %copy-start.3 = (f32[72,58]{0,1:T(8,128)S(1)}, f32[72,58]{0,1:T(8,128)}, u32[]{:S(2)}) copy-start(f32[72,58]{0,1:T(8,128)} %param.18) | copy-start | bytes 50116
  4.9 0.8 %copy-start.4 = (f32[2,72,32]{1,2,0:T(8,128)S(1)}, f32[2,72,32]{1,2,0:T(8,128)}, u32[]{:S(2)}) copy-start(f32[2,72,32]{1,2,0:T(8,128)} %param.19) | copy-start | bytes 55300
  5.6 0.7 copy-start.5
  6.4 0.7 copy-start.6
  7.1 0.7 copy-start.7
  7.8 0.7 copy-start.8

commit v7 on v5

--- a/solution.py
+++ b/solution.py
@@ -24,6 +24,8 @@
     ((a, b, c) for a in range(4) for b in range(4) for c in range(2)),
     key=lambda off: (-_hops(off), off),
 )
+NEAR = [(1, 1, 0), (3, 3, 0), (1, 0, 0), (3, 0, 0), (0, 1, 0), (0, 3, 0), (0, 0, 1), (0, 0, 0)]
+OFFSETS = [off for off in OFFSETS if off not in NEAR] + NEAR
 NBLK = len(OFFSETS)
 CHUNKS = 4
 PER = NBLK // CHUNKS
@@ -161,9 +163,9 @@
     tg[0:58, 0:72] = to_gcm[...]
     gsc[...] = jnp.zeros_like(gsc)
     gn[...] = jnp.zeros_like(gn)
-    xs[...] = jnp.zeros_like(xs)
-    x0[...] = jnp.zeros_like(x0)
-    s0[...] = jnp.zeros_like(s0)
+    xs[:, 48:64, :] = jnp.zeros((3 * PER, 16, 256), BF16)
+    x0[:, 48:64, :] = jnp.zeros((3 * PER, 16, 256), BF16)
+    s0[:, 56:64, :] = jnp.zeros((PER, 8, 256), F32)
     trt[...] = jnp.zeros_like(trt)
     for r in range(2):
         trt[r, :, 0:72] = tracer[r]
@@ -424,6 +426,31 @@
         for r in range(2):
             loop[r, 32 * s : 32 * s + 32, :] = rows[32 * r : 32 * r + 32]
 
+    to_smem.wait()
+    for load in loads:
+        load.wait()
+    for r in range(2):
+
+        def spot(s, carry):
+            at = pl.ds(r * 58 * STEP + slots_s[s, r, 0], 58, stride=STEP)
+            for t in range(3):
+                wide[t, at, :] = rbuf[s, _part(r, t), :].astype(F32)
+            return carry
+
+        lax.fori_loop(0, 32, spot, 0, unroll=4)
+        for part in range(2):
+            for level in range(29 * part, 29 * part + 29):
+                for t in range(3):
+                    at = (r * 58 + level) * STEP
+                    obuf[r, level, :, 128 * t : 128 * t + 128] = wide[t, at : at + 32, :].astype(BF16)
+            piece = pl.ds(29 * part, 29)
+            outs.append(
+                pltpu.make_async_copy(
+                    obuf.at[r, piece], state_out.at[r, piece], out_sem.at[2 * r + part]
+                )
+            )
+            outs[-1].start()
+
     cs[...] = jnp.zeros_like(cs)
     cf[...] = jnp.zeros_like(cf)
     cs[0:2, 0:72] = shift[...]
@@ -442,39 +469,8 @@
         result = (1.0 - weight) * pltpu.roll(now, 39, 0) + weight * now
         polar_v[r] = result[0:32, 0:72]
     outs.append(pltpu.make_async_copy(polar_v, polar_out, out_sem.at[5]))
-    outs[1].start()
-
-    to_smem.wait()
-    for q in range(4):
-        loads[q].wait()
-
-        def spot(s, carry):
-            for r in range(2):
-                at = pl.ds(r * 58 * STEP + slots_s[s, r, 0], 58, stride=STEP)
-                for t in range(3):
-                    wide[t, at, :] = rbuf[s, _part(r, t), :].astype(F32)
-            return carry
-
-        lax.fori_loop(8 * q, 8 * q + 8, spot, 0, unroll=2)
-
-    for r in range(2):
-        for part in range(2):
-
-            def narrow(level, carry):
-                for t in range(3):
-                    obuf[r, level, :, 128 * t : 128 * t + 128] = wide[
-                        t, pl.ds((r * 58 + level) * STEP, 32), :
-                    ].astype(BF16)
-                return carry
-
-            lax.fori_loop(29 * part, 29 * part + 29, narrow, 0, unroll=True)
-            piece = pl.ds(29 * part, 29)
-            outs.append(
-                pltpu.make_async_copy(
-                    obuf.at[r, piece], state_out.at[r, piece], out_sem.at[2 * r + part]
-                )
-            )
-            outs[-1].start()
+    outs[-1].start()
+
     for out in outs:
         out.wait()
 

time: 69.3 us -> 68.9 us (level)
  no operation moved by 1% of the time
where the time goes in v7:
time: 68.9 us; the launch traced here: 68.3 us
  Pallas kernels  67.7 us (98%)
    pallas_call x1, Pallas kernels, per_device(): pl.pallas_call(advance, out_shape=(jax.ShapeDtypeStruct((32, 348, 128), B...  60.7 us
    pallas_call x1, Pallas kernels, per_device(): pl.pallas_call(place, out_shape=(jax.ShapeDtypeStruct((2, 58, 32, 384), B...  6.95 us

profile of v7, /device:TPU:16, one launch (start us, length us, event | category | flops | bytes accessed | tf_op | source)
XLA Modules:
  0.0 68.3 jit_solution(7659740411138519308)
XLA Ops:
  0.6 60.7 %advance.1 = (bf16[32,348,128]{2,1,0:T(8,128)(2,1)}, bf16[32,4,16,128]{3,2,1,0:T(8,128)(2,1)}, s32[32,8,128]{2,1,0:T(8,128)}, f32[32,2,8,128]{3,2,1,0:T(8,128)}) custom-call(s32[2,32]{1,0:T(2,128)} %flags.1, s32[2,32]{1,0:T(2,128)} %plan_s.1, bf16[2,58,32,384]{3,2,1,0:T(8,128)(2,1)} %bitcast.7, bf16[2,6,32,72]{3,2,1,0:T(8,128)(2,1)} %bitcast.8, ...), custom_call_target="tpu_custom_call" | custom-call | tf_op jit(solution)/shard_map/advance/pallas_call | solution.py:495
  61.3 7.0 %place.1 = (bf16[2,58,32,384]{3,2,1,0:T(8,128)(2,1)}, f32[2,6,32,72]{3,2,1,0:T(8,128)}, f32[2,32,72]{2,1,0:T(8,128)}) custom-call(s32[2,32]{1,0:T(2,128)} %plan_s.1, bf16[32,348,128]{2,1,0:T(8,128)(2,1)} %get-tuple-element.10.recv, bf16[32,4,16,128]{3,2,1,0:T(8,128)(2,1)} %get-tuple-element.11.trec_hbm, s32[32,8,128]{2,1,0:T(8,128)} %get-tuple-element.12.prec_hbm, ...), custom_call_target="tpu_custom_call" | custom-call | tf_op jit(solution)/shard_map/place/pallas_call | solution.py:553

commit v8 on v7

--- a/solution.py
+++ b/solution.py
@@ -72,18 +72,25 @@
 
 def advance(
     flags,
+    plan_in,
+    crm,
+    gcm_in,
+    h_in,
+    v_in,
+    to_crm_in,
+    to_gcm_in,
+    tracer_in,
+    recv,
+    trec,
+    prec,
+    tend_out,
     plan_v,
-    crm,
     gcm,
     h_ref,
     v_ref,
     to_crm,
     to_gcm,
     tracer,
-    recv,
-    trec,
-    prec,
-    tend_out,
     tbuf,
     crm_v,
     cn,
@@ -107,6 +114,7 @@
     pack,
     order_v,
     order,
+    small_sem,
     in_sem,
     order_sem,
     self_sem,
@@ -119,6 +127,18 @@
     trsem,
 ):
     me = lax.axis_index("lon")
+    pairs = (
+        (plan_in, plan_v),
+        (h_in, h_ref),
+        (v_in, v_ref),
+        (to_crm_in, to_crm),
+        (to_gcm_in, to_gcm),
+        (tracer_in, tracer),
+        (gcm_in, gcm),
+    )
+    smalls = [pltpu.make_async_copy(a, b, small_sem.at[n]) for n, (a, b) in enumerate(pairs)]
+    for small in smalls:
+        small.start()
     loads = [pltpu.make_async_copy(crm.at[r], crm_v.at[r], in_sem.at[r]) for r in range(2)]
     for load in loads:
         load.start()
@@ -128,6 +148,7 @@
     for k in range(NBLK - 1):
         pl.semaphore_signal(barrier, inc=1, device_id={"lon": peers[k]}, device_id_type=MESH)
 
+    smalls[0].wait()
     for r in range(2):
         owners = jnp.broadcast_to(plan_v[r : r + 1, :] // 32, (32, 32))
         at = jnp.where(owners == _iota((32, 32), 0), _iota((32, 32), 1), 0)
@@ -149,6 +170,8 @@
     tile_v = _onehot(_iota((58, 256), 1) % 64 == _iota((58, 256), 0))
     tile_vt = _onehot(_iota((256, 58), 0) % 64 == _iota((256, 58), 1))
     diag = _iota((256, 256), 0) // 64 == _iota((256, 256), 1) // 64
+    smalls[1].wait()
+    smalls[2].wait()
     h_rep = _dot(_dot(tile_ht, h_ref[...]).astype(BF16), tile_h)
     v_rep = _dot(_dot(tile_vt, v_ref[...]).astype(BF16), tile_v)
     hbd[...] = jnp.where(diag, h_rep, 0.0).astype(BF16)
@@ -157,6 +180,8 @@
         spread[t] = _onehot(_iota((256, 256), 0) % 128 == _lane_map(_iota((256, 256), 1) // 64, lanes))
         hit = _iota((256, 128), 1) == _lane_map(_iota((256, 128), 0) // 64, lanes)
         gather[t * 256 : t * 256 + 256, :] = jnp.where(hit, jnp.float32(1.0 / 64), 0.0).astype(BF16)
+    for small in smalls[3:]:
+        small.wait()
     tc[...] = jnp.zeros_like(tc)
     tc[0:58, 0:72] = 0.5 * to_crm[...]
     tg[...] = jnp.zeros_like(tg)
@@ -500,9 +525,16 @@
             jax.ShapeDtypeStruct((32, 8, 128), jnp.int32),
             jax.ShapeDtypeStruct((32, 2, 8, 128), F32),
         ),
-        in_specs=[smem, vmem, hbm] + [vmem] * 6,
+        in_specs=[smem] + [hbm] * 8,
         out_specs=(hbm, hbm, hbm, hbm),
         scratch_shapes=[
+            pltpu.VMEM((2, 32), jnp.int32),
+            pltpu.VMEM((2, 6, 32, 72), BF16),
+            pltpu.VMEM((64, 64), BF16),
+            pltpu.VMEM((58, 58), BF16),
+            pltpu.VMEM((58, 72), F32),
+            pltpu.VMEM((58, 72), F32),
+            pltpu.VMEM((2, 32, 72), F32),
             pltpu.VMEM((32, 2, 8, 128), F32),
             pltpu.VMEM((2, 58, 32, 384), BF16),
             pltpu.VMEM((3, 2 * 58 * STEP, 128), F32),
@@ -526,6 +558,7 @@
             pltpu.VMEM((8, 128), jnp.int32),
             pltpu.VMEM((2, 32, 128), jnp.int32),
             pltpu.SMEM((2, 32, 128), jnp.int32),
+            dma((7,)),
             dma((2,)),
             dma,
             dma,

time: 68.9 us -> 68.9 us (level)
  no operation moved by 1% of the time
where the time goes in v8:
time: 68.9 us; the launch traced here: 68.3 us
  Pallas kernels  67.7 us (98%)
    pallas_call x1, Pallas kernels, per_device(): pl.pallas_call(advance, out_shape=(jax.ShapeDtypeStruct((32, 348, 128), B...  60.7 us
    pallas_call x1, Pallas kernels, per_device(): pl.pallas_call(place, out_shape=(jax.ShapeDtypeStruct((2, 58, 32, 384), B...  6.95 us

profile of v8, /device:TPU:16, one launch (start us, length us, event | category | flops | bytes accessed | tf_op | source)
XLA Modules:
  0.0 68.3 jit_solution(15648811377677359548)
XLA Ops:
  0.6 60.7 %advance.1 = (bf16[32,348,128]{2,1,0:T(8,128)(2,1)}, bf16[32,4,16,128]{3,2,1,0:T(8,128)(2,1)}, s32[32,8,128]{2,1,0:T(8,128)}, f32[32,2,8,128]{3,2,1,0:T(8,128)}) custom-call(s32[2,32]{1,0:T(2,128)} %flags.1, s32[2,32]{1,0:T(2,128)} %plan_s.1, bf16[2,58,32,384]{3,2,1,0:T(8,128)(2,1)} %bitcast.7, bf16[2,6,32,72]{3,2,1,0:T(8,128)(2,1)} %bitcast.8, ...), custom_call_target="tpu_custom_call" | custom-call | tf_op jit(solution)/shard_map/advance/pallas_call | solution.py:520
  61.4 7.0 %place.1 = (bf16[2,58,32,384]{3,2,1,0:T(8,128)(2,1)}, f32[2,6,32,72]{3,2,1,0:T(8,128)}, f32[2,32,72]{2,1,0:T(8,128)}) custom-call(s32[2,32]{1,0:T(2,128)} %plan_s.1, bf16[32,348,128]{2,1,0:T(8,128)(2,1)} %get-tuple-element.10.recv, bf16[32,4,16,128]{3,2,1,0:T(8,128)(2,1)} %get-tuple-element.11.trec_hbm, s32[32,8,128]{2,1,0:T(8,128)} %get-tuple-element.12.prec_hbm, ...), custom_call_target="tpu_custom_call" | custom-call | tf_op jit(solution)/shard_map/place/pallas_call | solution.py:586
